TPU v7x, 512 devices: a whole 4x4x16 slice. The times are simulated.
512 devices in a mesh: stream: 32 (over z, core), girth: 16 (over y, x).
Axes of the slice: x: 4, y: 4, z: 16, core: 2. Of those that a mesh axis runs over, the one named last changes fastest.
Arguments:
- state: float32 [64, 7, 128, 128], P('stream', None, 'girth'), may hold values from -1.8 to 1.8
- propeller: float32 [7, 131072], P(None, ('stream', 'girth')), may hold values from -6 to 6
- donor_index: int32 [512, 128], P(('stream', 'girth')), may hold values from -1 to 255, as said below
- fringe_index: int32 [512, 128], P(('stream', 'girth')), may hold values from -1 to 2047, as said below
- donor_weight: float32 [512, 128], P(('stream', 'girth')), may hold values from 0.25 to 1
- disk_mask: int32 [64, 128, 128], P('stream', 'girth'), may hold values 0 or 1
- thrust: float32 [7], replicated, may hold values from -1.8 to 1.8
- face: float32 [64, 6, 128, 128], P('stream', None, 'girth'), may hold values from 0.2 to 1
- coupling: float32 [6, 7, 7], replicated, may hold values from -0.875 to 0.875
- diag_inverse: bfloat16 [64, 7, 7, 128, 128], P('stream', None, None, 'girth'), may hold values from -0.15039062 to 1
- lower_jacobian: float32 [7, 7], replicated, may hold values from -0.06 to 1.06
- upper_jacobian: float32 [7, 7], replicated, may hold values from -0.06 to 1.06
Outputs:
- new_state: float32 [64, 7, 128, 128], P('stream', None, 'girth')
- residual: float32 [64, 7, 128, 128], P('stream', None, 'girth')
Inputs may be any that keep to these rules, and one draw needn't show every extreme that they name: `donor_index`: live slots of one device and peer come first; every device of one streamwise index fills all 8 slots toward one common peer. `fringe_index`: equal to -1 exactly where donor_index is -1.
All inputs are finite; a program needn't handle non-finite values. No bound on the sum of `disk_mask` on one device may be relied on, other than what follows from the above.
Results may differ from a plain program's by a relative error of at most 0.0003.
Values sent between devices are 32-bit elements; how exact they have to be, the bound alone decides.
No kernel may reach another device: no remote copies, remote signals or barrier semaphores. Data moves between devices by JAX's collectives and lax.ppermute only.
A program may use at most 64 MiB of HBM per device.

v0:
```python
import jax
import jax.numpy as jnp
from jax import lax
from jax.sharding import PartitionSpec as P

PRECISE = lax.Precision.HIGHEST


def extended(block, sides, width, periodic):
    for axis, dim in sides:
        count = lax.axis_size(axis)
        forward = [(i, i + 1) for i in range(count - 1)]
        if periodic:
            forward.append((count - 1, 0))
        backward = [(target, source) for source, target in forward]
        low = lax.ppermute(
            lax.slice_in_dim(block, block.shape[dim] - width, None, axis=dim), axis, forward
        )
        high = lax.ppermute(lax.slice_in_dim(block, 0, width, axis=dim), axis, backward)
        block = jnp.concatenate([low, block, high], axis=dim)
    return block


def prefix(shard, axis, combine, identity, reverse):
    count, place = (lax.axis_size(axis), lax.axis_index(axis))
    everything = jax.tree.map(lambda part: lax.all_gather(part, axis), shard)
    start = jax.tree.map(
        lambda part, zero: jnp.broadcast_to(jnp.asarray(zero, part.dtype), part.shape),
        shard,
        identity,
    )

    def turn(k, before):
        at = count - 1 - k if reverse else k
        reached = at > place if reverse else at < place
        new = combine(before, jax.tree.map(lambda part: part[at], everything))
        return jax.tree.map(lambda a, b: jnp.where(reached, a, b), new, before)

    return lax.fori_loop(0, count, turn, start)


def residual_from(current, stream_pad, beside_all, face, coupling, disk_mask, thrust):
    normal_pad = jnp.pad(current, ((0, 0), (0, 0), (0, 0), (1, 1)))
    beside = [
        stream_pad[:-2],
        stream_pad[2:],
        beside_all[:, :, :-2],
        beside_all[:, :, 2:],
        normal_pad[..., :-2],
        normal_pad[..., 2:],
    ]
    residual = disk_mask.astype(jnp.float32)[:, None] * thrust[None, :, None, None]
    for direction in range(6):
        residual = residual + face[:, direction : direction + 1] * jnp.einsum(
            "ij,ajbc->aibc", coupling[direction], beside[direction] - current, precision=PRECISE
        )
    return residual


def forward_step(matrix):

    def advance(previous, inputs):
        inverse, source = inputs
        inverse = inverse.astype(jnp.float32)
        result = jnp.einsum(
            "ijc,jc->ic",
            inverse,
            source + jnp.dot(matrix, previous, precision=PRECISE),
            precision=PRECISE,
        )
        return (result, result)

    return advance


def backward_step(matrix):

    def advance(following, inputs):
        inverse, star = inputs
        inverse = inverse.astype(jnp.float32)
        result = star + jnp.einsum(
            "ijc,jc->ic", inverse, jnp.dot(matrix, following, precision=PRECISE), precision=PRECISE
        )
        return (result, result)

    return advance


def unit_maps(columns):
    return jnp.broadcast_to(jnp.eye(7, dtype=jnp.float32)[:, :, None], (7, 7, columns))


def forward_maps(inverse, source, matrix):

    def advance(carried, inputs):
        compound, start_offset = carried
        block, term = inputs
        block = block.astype(jnp.float32)
        factor = jnp.einsum("ijc,jk->ikc", block, matrix, precision=PRECISE)
        compound = jnp.einsum("ijc,jkc->ikc", factor, compound, precision=PRECISE)
        start_offset = jnp.einsum(
            "ijc,jc->ic",
            block,
            term + jnp.dot(matrix, start_offset, precision=PRECISE),
            precision=PRECISE,
        )
        return ((compound, start_offset), None)

    columns = source.shape[2]
    start = (unit_maps(columns), jnp.zeros((7, columns), jnp.float32))
    result, _ = lax.scan(advance, start, (inverse, source))
    return result


def backward_maps(inverse, stars, matrix):

    def advance(carried, inputs):
        compound, start_offset = carried
        block, star = inputs
        block = block.astype(jnp.float32)
        factor = jnp.einsum("ijc,jk->ikc", block, matrix, precision=PRECISE)
        compound = jnp.einsum("ijc,jkc->ikc", factor, compound, precision=PRECISE)
        start_offset = star + jnp.einsum(
            "ijc,jc->ic", block, jnp.dot(matrix, start_offset, precision=PRECISE), precision=PRECISE
        )
        return ((compound, start_offset), None)

    columns = stars.shape[2]
    start = (unit_maps(columns), jnp.zeros((7, columns), jnp.float32))
    result, _ = lax.scan(advance, start, (inverse, stars), reverse=True)
    return result


def compose(earlier, later_map):
    return (
        jnp.einsum("ijc,jkc->ikc", later_map[0], earlier[0], precision=PRECISE),
        jnp.einsum("ijc,jc->ic", later_map[0], earlier[1], precision=PRECISE) + later_map[1],
    )


def identity_of(maps):
    return (unit_maps(maps[1].shape[1]), jnp.zeros_like(maps[1]))


def sweep_pair(inverse, source, lower, upper, forward_chain, backward_chain):
    maps = forward_maps(inverse, source, lower)
    entry = forward_chain(maps)[1]
    _, stars = lax.scan(forward_step(lower), entry, (inverse, source))
    later_maps = backward_maps(inverse, stars, upper)
    exit_value = backward_chain(later_maps)[1]
    _, updates = lax.scan(backward_step(upper), exit_value, (inverse, stars), reverse=True)
    return updates


def per_device(
    state,
    propeller,
    donor_index,
    fringe_index,
    donor_weight,
    disk_mask,
    thrust,
    face,
    coupling,
    diag_inverse,
    lower_jacobian,
    upper_jacobian,
):
    row_count, var_count, girth_cells, normal_cells = state.shape
    columns = girth_cells * normal_cells
    cell_count = row_count * columns
    is_live = donor_index >= 0
    outgoing = jnp.take(propeller, jnp.maximum(donor_index[0], 0), axis=1) * jnp.where(
        is_live, donor_weight, 0.0
    )
    target = jnp.where(is_live, fringe_index, -1)
    incoming, landing = (
        lax.all_to_all(outgoing, "girth", split_axis=1, concat_axis=1, tiled=True),
        lax.all_to_all(target, "girth", split_axis=1, concat_axis=1, tiled=True),
    )
    flat_index = jnp.where(landing[0] >= 0, landing[0], cell_count)
    accumulated = (
        jnp.zeros((cell_count, var_count), jnp.float32).at[flat_index].add(incoming.T, mode="drop")
    )
    hit_count = jnp.zeros((cell_count,), jnp.int32).at[flat_index].add(1, mode="drop")
    fringe = (hit_count > 0).reshape(row_count, 1, girth_cells, normal_cells)
    donated = accumulated.reshape(row_count, girth_cells, normal_cells, var_count).transpose(
        0, 3, 1, 2
    )
    current = jnp.where(fringe, donated, state)
    stream_pad = extended(current, (("stream", 0),), 1, False)
    beside_all = extended(current, (("girth", 2),), 1, True)
    residual = residual_from(current, stream_pad, beside_all, face, coupling, disk_mask, thrust)
    source = jnp.where(fringe, 0.0, -residual).reshape(row_count, var_count, columns)
    inverse = diag_inverse.reshape(row_count, var_count, var_count, columns)

    def forward_chain(maps):
        return prefix(maps, "stream", compose, identity_of(maps), False)

    def backward_chain(maps):
        return prefix(maps, "stream", compose, identity_of(maps), True)

    updates = sweep_pair(
        inverse, source, lower_jacobian, upper_jacobian, forward_chain, backward_chain
    )
    new_state = current + updates.reshape(row_count, var_count, girth_cells, normal_cells)
    return (new_state, residual)


def solution(mesh):
    placed = (
        P("stream", None, "girth", None),
        P(None, ("stream", "girth")),
        P(("stream", "girth"), None),
        P(("stream", "girth"), None),
        P(("stream", "girth"), None),
        P("stream", "girth", None),
        P(),
        P("stream", None, "girth", None),
        P(),
        P("stream", None, None, "girth", None),
        P(),
        P(),
    )
    return jax.shard_map(
        per_device,
        mesh=mesh,
        in_specs=placed,
        out_specs=(P("stream", None, "girth", None), P("stream", None, "girth", None)),
        check_vma=False,
    )
```

profile of v0, /device:TPU:1, one launch (start us, length us, event | category | flops | bytes accessed | tf_op | source)
XLA Modules:
  0.0 369.3 jit_solution(1793871304822750274)
XLA Ops:
  8.6 7.6 %all-to-all-start = ((s32[1,16,8]{2,0,1:T(1,128)}), s32[1,16,8]{2,0,1:T(1,128)S(1)}, u32[]{:S(2)}, u32[]{:S(2)}) async-start(s32[1,16,8]{2,0,1:T(1,128)} %bitcast.29), calls=%async_computation | async-start | bytes 16384 | tf_op jit(solution)/shard_map/all_to_all | solution.py:179
  21.4 1.2 reshape.153
  23.4 6.7 %all-to-all-start.1 = ((f32[7,16,8]{0,2,1:T(8,128)}), f32[7,16,8]{0,2,1:T(8,128)S(1)}, u32[]{:S(2)}, u32[]{:S(2)}) async-start(f32[7,16,8]{0,2,1:T(8,128)} %fusion.49), calls=%async_computation.1 | async-start | bytes 131072 | tf_op jit(solution)/shard_map/all_to_all | solution.py:178
  31.4 1.2 scatter_custom_fusion
  32.6 3.9 %all-to-all-done.1 = f32[7,16,8]{0,2,1:T(8,128)S(1)} async-done(((f32[7,16,8]{0,2,1:T(8,128)}), f32[7,16,8]{0,2,1:T(8,128)S(1)}, u32[]{:S(2)}, u32[]{:S(2)}) %all-to-all-start.1) | async-done | bytes 3616 | tf_op jit(solution)/shard_map/all_to_all | solution.py:178
  36.6 1.3 scatter_custom_fusion.1
  39.0 6.1 %collective-permute-start = (f32[1,7,8,128]{3,1,2,0:T(8,128)S(1)}, f32[1,7,8,128]{3,1,2,0:T(8,128)S(1)}, u32[]{:S(2)}, u32[]{:S(2)}) collective-permute-start(f32[1,7,8,128]{3,1,2,0:T(8,128)S(1)} %get-tuple-element.730), channel_id=1, source_target_pairs={{0,16},{16,32},{32,48},{48,64},{64,80},{80,96},{96,112},{112,128},... | collective-permute-start | bytes 86024 | tf_op jit(solution)/shard_map/ppermute | solution.py:16
  45.1 1.9 collective-permute-start.1
  47.1 2.2 collective-permute-start.2
  49.3 6.4 %collective-permute-start.3 = (f32[2,7,1,128]{3,1,2,0:T(8,128)S(1)}, f32[2,7,1,128]{3,1,2,0:T(8,128)S(1)}, u32[]{:S(2)}, u32[]{:S(2)}) collective-permute-start(f32[2,7,1,128]{3,1,2,0:T(8,128)S(1)} %get-tuple-element.727), channel_id=1, source_target_pairs={{1,0},{2,1},{3,2},{4,3},{5,4},{6,5},{7,6},{8,7},{9,8},{10,9},{11,1... | collective-permute-start | bytes 21512 | tf_op jit(solution)/shard_map/ppermute | solution.py:19
  59.2 2.2 broadcast_in_dim.86.clone
  61.4 31.2 %while.87 = (s32[]{:T(128)}, f32[7,7,1024]{1,0,2:T(8,128)}, f32[7,1024]{0,1:T(8,128)S(1)}, bf16[2,7,7,1024]{3,2,1,0:T(8,128)(2,1)S(1)}, f32[7,7]{0,1:T(8,128)S(1)}, /*index=5*/f32[2,7,1024]{2,1,0:T(8,128)S(1)}, s32[]{:T(128)}) while((s32[]{:T(128)}, f32[7,7,1024]{1,0,2:T(8,128)}, f32[7,1024]{0,1:T(8,128)S(1)}, ...), condition=%wide.region_3.4_spmd, body=%wide.region_2.3_spmd.sunk | while | flops 9182210 | bytes 2828601 | solution.py:111
  62.6 2.7 copy.110
  65.3 2.3 copy.169
  67.6 1.1 copy-done
  68.7 8.3 %convolution_bitcast_fusion.13 = f32[7,7,1024]{1,0,2:T(8,128)} fusion(f32[7,7,1024]{0,1,2:T(8,128)S(1)} %copy-done, f32[7,7,1024]{1,0,2:T(8,128)S(1)} %copy.169), kind=kOutput, calls=%fused_computation.3.clone.1 | convolution fusion | flops 4214784 | bytes 602112 | tf_op jit(solution)/shard_map/while/body/eval_jaxpr/ijc,jkc->ikc/dot_general | solution.py:100
  78.2 2.7 copy.110
  80.9 2.3 copy.169
  83.2 1.1 copy-done
  84.3 8.3 %convolution_bitcast_fusion.13 = f32[7,7,1024]{1,0,2:T(8,128)} fusion(f32[7,7,1024]{0,1,2:T(8,128)S(1)} %copy-done, f32[7,7,1024]{1,0,2:T(8,128)S(1)} %copy.169), kind=kOutput, calls=%fused_computation.3.clone.1 | convolution fusion | flops 4214784 | bytes 602112 | tf_op jit(solution)/shard_map/while/body/eval_jaxpr/ijc,jkc->ikc/dot_general | solution.py:100
  92.6 3.5 copy.45
  96.5 40.8 %all-gather.4 = f32[32,7,1024]{2,1,0:T(8,128)S(1)} all-gather(f32[1,7,1024]{2,1,0:T(8,128)S(1)} %bitcast.304), channel_id=3, replica_groups=mesh['stream'=32,'girth'=16] {'stream'}, dimensions={0}, use_global_device_ids=true | all-gather | bytes 946176 | tf_op jit(solution)/shard_map/all_gather | solution.py:26
  137.3 43.4 %all-gather.9.cloned.1.call-done = f32[224,7,1024]{2,1,0:T(8,128)} async-done(((f32[7,7,1024]{2,1,0:T(8,128)}), f32[224,7,1024]{2,1,0:T(8,128)}) %all-gather.9.cloned.1.call-update) | async-done | bytes 6422544 | tf_op jit(solution)/shard_map/all_gather | solution.py:26
  180.7 34.4 %while.90 = (s32[]{:T(128)}, f32[7,1024]{1,0:T(8,128)S(1)}, s32[]{:T(128)}, f32[32,7,7,1024]{3,2,1,0:T(8,128)}, f32[32,7,1024]{2,1,0:T(8,128)S(1)}, /*index=5*/s32[]{:T(128)}, s32[]{:T(128)}) while((s32[]{:T(128)}, f32[7,1024]{1,0:T(8,128)S(1)}, s32[]{:T(128)}, f32[32,7,7,1024]{3,2,1,0:T(8,128)}, f32[32,7,1024]{2,1,0:T(8,128)S(1)}, ...), condition=%wide.region_5.6_spmd.clone, body=%wide.region_4.5_spmd.clone.sunk | while | flops 121860 | bytes 430186 | solution.py:39
  215.7 2.2 broadcast_in_dim.86
  217.9 30.1 %while.91 = (s32[]{:T(128)}, f32[7,7,1024]{1,0,2:T(8,128)}, f32[7,1024]{1,0:T(8,128)S(1)}, bf16[2,7,7,1024]{3,2,1,0:T(8,128)(2,1)S(1)}, f32[7,7]{0,1:T(8,128)S(1...) while((s32[]{:T(128)}, f32[7,7,1024]{1,0,2:T(8,128)}, f32[7,1024]{1,0:T(8,128)S(1)}, ...), condition=%wide.region_9.10_spmd.clone, body=%wide.region_8.9_spmd.clone.sunk | while | flops 9189380 | bytes 2828631 | solution.py:130
  218.5 2.7 copy.112
  221.2 2.3 copy.170
  223.5 1.1 copy-done.1
  224.7 8.3 %convolution_bitcast_fusion.16 = f32[7,7,1024]{1,0,2:T(8,128)} fusion(f32[7,7,1024]{0,1,2:T(8,128)S(1)} %copy-done.1, f32[7,7,1024]{1,0,2:T(8,128)S(1)} %copy.170), kind=kOutput, calls=%fused_computation.25.clone.1 | convolution fusion | flops 4214784 | bytes 602112 | tf_op jit(solution)/shard_map/while/body/eval_jaxpr/ijc,jkc->ikc/dot_general | solution.py:122
  233.6 2.7 copy.112
  236.3 2.3 copy.170
  238.6 1.1 copy-done.1
  239.7 8.3 %convolution_bitcast_fusion.16 = f32[7,7,1024]{1,0,2:T(8,128)} fusion(f32[7,7,1024]{0,1,2:T(8,128)S(1)} %copy-done.1, f32[7,7,1024]{1,0,2:T(8,128)S(1)} %copy.170), kind=kOutput, calls=%fused_computation.25.clone.1 | convolution fusion | flops 4214784 | bytes 602112 | tf_op jit(solution)/shard_map/while/body/eval_jaxpr/ijc,jkc->ikc/dot_general | solution.py:122
  248.0 3.4 copy.50
  252.2 36.0 %all-gather.5 = f32[32,7,1024]{2,1,0:T(8,128)S(1)} all-gather(f32[1,7,1024]{2,1,0:T(8,128)S(1)} %bitcast.301), channel_id=5, replica_groups=mesh['stream'=32,'girth'=16] {'stream'}, dimensions={0}, use_global_device_ids=true | all-gather | bytes 946176 | tf_op jit(solution)/shard_map/all_gather | solution.py:26
  288.2 38.3 %all-gather.11.cloned.1.call-done = f32[224,7,1024]{2,1,0:T(8,128)} async-done(((f32[7,7,1024]{2,1,0:T(8,128)}), f32[224,7,1024]{2,1,0:T(8,128)}) %all-gather.11.cloned.1.call-update) | async-done | bytes 6422544 | tf_op jit(solution)/shard_map/all_gather | solution.py:26
  326.5 34.7 %while.92 = (s32[]{:T(128)}, f32[7,1024]{1,0:T(8,128)S(1)}, s32[]{:T(128)}, f32[32,7,7,1024]{3,2,1,0:T(8,128)}, f32[32,7,1024]{2,1,0:T(8,128)S(1)}, /*index=5*/s32[]{:T(128)}, s32[]{:T(128)}, s32[]{:T(128)}, s32[]{:T(128)}) while((s32[]{:T(128)}, f32[7,1024]{1,0:T(8,128)S(1)}, s32[]{:T(128)}, f32[32,7,7,1024]{3,2,1,0:T(8,128)}, ...), condition=%wide.region_11.12_spmd.clone, body=%wide.region_10.11_spmd.clone.sunk | while | flops 121864 | bytes 430248 | solution.py:39
  330.8 1.0 fusion.129
  331.9 1.0 fusion.129
  333.0 1.0 fusion.129
  334.1 1.0 fusion.129
  335.2 1.0 fusion.129
  336.3 1.0 fusion.129
  337.3 1.0 fusion.129
  340.6 1.0 fusion.129
  341.7 1.0 fusion.129
  342.8 1.0 fusion.129
  (273 shorter events, 76.8 us)
Async XLA Ops:
  7.2 51.2 %copy-start.4 = (f32[6,7,7]{2,1,0:T(8,128)S(1)}, f32[6,7,7]{2,1,0:T(8,128)}, u32[]{:S(2)}) copy-start(f32[6,7,7]{2,1,0:T(8,128)} %param.32) | copy-start | bytes 3532
  8.6 14.8 %all-to-all-start = ((s32[1,16,8]{2,0,1:T(1,128)}), s32[1,16,8]{2,0,1:T(1,128)S(1)}, u32[]{:S(2)}, u32[]{:S(2)}) async-start(s32[1,16,8]{2,0,1:T(1,128)} %bitcast.29), calls=%async_computation | async-start | bytes 16384 | tf_op jit(solution)/shard_map/all_to_all | solution.py:179
  23.4 13.2 %all-to-all-start.1 = ((f32[7,16,8]{0,2,1:T(8,128)}), f32[7,16,8]{0,2,1:T(8,128)S(1)}, u32[]{:S(2)}, u32[]{:S(2)}) async-start(f32[7,16,8]{0,2,1:T(8,128)} %fusion.49), calls=%async_computation.1 | async-start | bytes 131072 | tf_op jit(solution)/shard_map/all_to_all | solution.py:178
  30.0 150.6 %all-gather.9.cloned.1.call-start = ((), (), s32[]{:S(2)}) async-start(), calls=%async_computation.2 | async-start | bytes 7569408 | tf_op jit(solution)/shard_map/all_gather | solution.py:26
  39.0 16.7 %collective-permute-start = (f32[1,7,8,128]{3,1,2,0:T(8,128)S(1)}, f32[1,7,8,128]{3,1,2,0:T(8,128)S(1)}, u32[]{:S(2)}, u32[]{:S(2)}) collective-permute-start(f32[1,7,8,128]{3,1,2,0:T(8,128)S(1)} %get-tuple-element.730), channel_id=1, source_target_pairs={{0,16},{16,32},{32,48},{48,64},{64,80},{80,96},{96,112},{112,128},... | collective-permute-start | bytes 86024 | tf_op jit(solution)/shard_map/ppermute | solution.py:16
  45.1 11.5 %collective-permute-start.1 = (f32[1,7,8,128]{3,1,2,0:T(8,128)S(1)}, f32[1,7,8,128]{3,1,2,0:T(8,128)S(1)}, u32[]{:S(2)}, u32[]{:S(2)}) collective-permute-start(f32[1,7,8,128]{3,1,2,0:T(8,128)S(1)} %get-tuple-element.729), channel_id=1, source_target_pairs={{16,0},{32,16},{48,32},{64,48},{80,64},{96,80},{112,96},{128,112},... | collective-permute-start | bytes 86024 | tf_op jit(solution)/shard_map/ppermute | solution.py:19
  47.1 10.4 %collective-permute-start.2 = (f32[2,7,1,128]{3,1,2,0:T(8,128)S(1)}, f32[2,7,1,128]{3,1,2,0:T(8,128)S(1)}, u32[]{:S(2)}, u32[]{:S(2)}) collective-permute-start(f32[2,7,1,128]{3,1,2,0:T(8,128)S(1)} %get-tuple-element.728), channel_id=1, source_target_pairs={{0,1},{1,2},{2,3},{3,4},{4,5},{5,6},{6,7},{7,8},{8,9},{9,10},{10,1... | collective-permute-start | bytes 21512 | tf_op jit(solution)/shard_map/ppermute | solution.py:16
  49.3 9.1 %collective-permute-start.3 = (f32[2,7,1,128]{3,1,2,0:T(8,128)S(1)}, f32[2,7,1,128]{3,1,2,0:T(8,128)S(1)}, u32[]{:S(2)}, u32[]{:S(2)}) collective-permute-start(f32[2,7,1,128]{3,1,2,0:T(8,128)S(1)} %get-tuple-element.727), channel_id=1, source_target_pairs={{1,0},{2,1},{3,2},{4,3},{5,4},{6,5},{7,6},{8,7},{9,8},{10,9},{11,1... | collective-permute-start | bytes 21512 | tf_op jit(solution)/shard_map/ppermute | solution.py:19
  65.3 3.4 copy-start
  80.9 3.4 copy-start
  92.6 3.6 copy-start.3
  92.6 122.5 %copy-start.2 = (f32[7,7]{1,0:T(8,128)S(1)}, f32[7,7]{1,0:T(8,128)}, u32[]{:S(2)}) copy-start(f32[7,7]{1,0:T(8,128)} %param.34) | copy-start | bytes 592
  96.1 230.4 %all-gather.11.cloned.1.call-start = ((), (), s32[]{:S(2)}) async-start(), calls=%async_computation.3 | async-start | bytes 7569408 | tf_op jit(solution)/shard_map/all_gather | solution.py:26
  221.2 3.4 copy-start.1
  236.3 3.4 copy-start.1
Sparse Core Ops, SparseCore 0:
  96.2 84.3 all-gather.8
  251.6 74.7 all-gather.10
where the time goes:
time: 372 us; the launch traced here: 369 us
  waiting for transfers between devices  85.6 us (23%)
  blocking collectives  76.8 us (21%)
  other arithmetic  74.7 us (20%)
  local copies, waits for them, and re-layouts  44 us (12%)
  matrix products  39.8 us (11%)
  starting transfers between devices  30.9 us (8%)
  between operations  14.4 us (4%)
    all_gather x2, waiting for transfers between devices, prefix(): everything = jax.tree.map(lambda part: lax.all_gather(part, axis), shard)  81.7 us
    all_gather x2, blocking collectives, prefix(): everything = jax.tree.map(lambda part: lax.all_gather(part, axis), shard)  76.8 us
    dot_general x64, other arithmetic, compose(): jnp.einsum('ijc,jc->ic', later_map[0], earlier[1], precision=PRECISE)  65.1 us
    dot_general x4, matrix products, advance(): compound = jnp.einsum('ijc,jkc->ikc', factor, compound, precision=PRECISE)  33.3 us
    while x12, local copies, waits for them, and re-layouts  13.8 us
    dot_general x4, local copies, waits for them, and re-layouts, advance(): factor = jnp.einsum('ijc,jk->ikc', block, matrix, precision=PRECISE)  10.8 us
    ppermute x2, starting transfers between devices, extended(): lax.ppermute(lax.slice_in_dim(block, 0, width, axis=dim), axis, backward)  8.33 us
    ppermute x2, starting transfers between devices, extended(): lax.ppermute(lax.slice_in_dim(block, block.shape[dim] - width, None, axis...  8.29 us
  transfers between devices with their start and end apart: 8, of which 3 were waited for; matrix products, arithmetic and copies ran while one was open for 4% of the time, Pallas kernels for 0%

commit v1 on v0

v1 whole, which is shorter than its diff:
```python
import jax
import jax.numpy as jnp
from jax import lax
from jax.experimental import pallas as pl
from jax.experimental.pallas import tpu as pltpu
from jax.sharding import PartitionSpec as P

F32 = jnp.float32
BF16 = jnp.bfloat16
VARS = 7
STREAMS = 32
GIRTHS = 16
DONOR_ROWS = 24
SEND_ROWS = 33
BACK_ROWS = 7
FLOW_VALUES = 32


def lanes(shape=(8, 128)):
    return lax.broadcasted_iota(jnp.int32, shape, len(shape) - 1)


def sublanes(shape=(8, 128)):
    return lax.broadcasted_iota(jnp.int32, shape, len(shape) - 2)


def split_parts(x):
    high = x.astype(BF16).astype(F32)
    rest = x - high
    middle = rest.astype(BF16).astype(F32)
    return high, middle, rest - middle


def block_transpose(a, b, c, d):
    lane = lanes()
    half = lane < 64
    even = (lane & 32) == 0
    a, c = jnp.where(half, a, pltpu.roll(c, 64, 1)), jnp.where(half, pltpu.roll(a, 64, 1), c)
    b, d = jnp.where(half, b, pltpu.roll(d, 64, 1)), jnp.where(half, pltpu.roll(b, 64, 1), d)
    a, b = jnp.where(even, a, pltpu.roll(b, 32, 1)), jnp.where(even, pltpu.roll(a, 96, 1), b)
    c, d = jnp.where(even, c, pltpu.roll(d, 32, 1)), jnp.where(even, pltpu.roll(c, 96, 1), d)
    return a, b, c, d


def donor_kernel(prop_ref, index_ref, fringe_ref, weight_ref, state_ref, out_ref):
    place = lax.axis_index("girth")
    index = index_ref[...]
    cells = lax.broadcasted_iota(jnp.int32, (256, 128), 0)
    pick = jnp.where(cells == index, 1.0, 0.0).astype(BF16)
    values = jnp.zeros((VARS, 128), F32)
    for part in split_parts(prop_ref[...]):
        values = values + jnp.dot(part.astype(BF16), pick, preferred_element_type=F32)
    values = values * weight_ref[...]
    target = jnp.where(index >= 0, fringe_ref[...], -1).astype(F32)
    edges = [
        (
            state_ref[pl.ds(row * 56, VARS, stride=8), :],
            state_ref[pl.ds(row * 56 + 7, VARS, stride=8), :],
        )
        for row in range(2)
    ]
    upper = lax.rem(place + 1, GIRTHS)
    for peer in range(GIRTHS):
        start = peer * DONOR_ROWS
        out_ref[start : start + VARS, :] = values
        out_ref[start + VARS : start + 8, :] = target
        out_ref[start + 8 : start + 24, :] = jnp.zeros((16, 128), F32)
        for row, (first, last) in enumerate(edges):
            at = start + 8 + row * 8
            out_ref[at : at + VARS, :] = jnp.where(upper == peer, last, first)


def fringe_sums(landed_ref, place):
    sub, lane = sublanes(), lanes()
    row = lanes((1, 128))
    slot = row & 31
    left = {}
    right = []
    for group in range(4):
        entries = jnp.zeros((8, 128), F32)
        for quarter in range(4):
            sender = group * 4 + quarter
            shift = lax.rem(32 * quarter + 8 - 8 * place + 128, 128)
            rolled = pltpu.roll(landed_ref[sender * DONOR_ROWS : sender * DONOR_ROWS + 8, :], shift, 1)
            entries = jnp.where((lane >> 5) == quarter, rolled, entries)
        target = entries[7:8, :].astype(jnp.int32)
        live = target >= 0
        tall = target >> 7
        own = jnp.where(live & (slot >= 8) & (slot < 16), tall, -1)
        low = jnp.where(live & (slot < 8) & ((tall & 7) == 7), tall >> 3, -1)
        high = jnp.where(live & (slot >= 16) & (slot < 24) & ((tall & 7) == 0), tall >> 3, -1)
        onto = lax.broadcasted_iota(jnp.int32, (128, 128), 0)
        right.append(jnp.where(onto == (target & 127), 1.0, 0.0).astype(BF16))
        parts = split_parts(entries)
        for which, part in enumerate(parts):
            counted = 1.0 if which == 0 else 0.0
            marked = jnp.where(sub == 7, counted, part)
            rows = []
            for r in range(2):
                inside = own == sub + 8 * r
                for v in range(8):
                    rows.append(jnp.where(inside, marked[v : v + 1, :], 0.0))
            for side in (low, high):
                for r in range(2):
                    rows.append(jnp.where(side == r, marked, 0.0))
            left[which, group] = jnp.concatenate(rows, axis=0).astype(BF16)
    right = jnp.concatenate(right, axis=1)
    total = None
    for which in range(3):
        lhs = jnp.concatenate([left[which, group] for group in range(4)], axis=1)
        part = lax.dot_general(lhs, right, (((1,), (1,)), ((), ())), preferred_element_type=F32)
        total = part if total is None else total + part
    return total


def flow_kernel(
    landed_ref,
    state_ref,
    face_ref,
    disk_ref,
    diag_ref,
    thrust_ref,
    coupling_ref,
    send_ref,
    current_ref,
):
    place = lax.axis_index("girth")
    sub, lane = sublanes(), lanes()
    sums = fringe_sums(landed_ref, place)
    edges = []
    for side, peer in enumerate((lax.rem(place + 15, GIRTHS), lax.rem(place + 1, GIRTHS))):
        both = []
        for r in range(2):
            start = pl.multiple_of(peer * DONOR_ROWS + 8 + 8 * r, 8)
            edge = landed_ref[pl.ds(start, 8), :]
            found = sums[128 + side * 16 + r * 8 : 136 + side * 16 + r * 8, :]
            both.append(jnp.where(found[7:8, :] > 0.5, found, edge))
        edges.append(both)
    current, fringe = [], []
    for r in range(2):
        block = sums[r * 64 : (r + 1) * 64, :]
        hit = block[56:64, :] > 0.5
        fringe.append(hit)
        current.append(
            [jnp.where(hit, block[v * 8 : v * 8 + 8, :], state_ref[r, v]) for v in range(VARS)]
        )
    zero = jnp.zeros((8, 128), F32)
    residual = []
    for r in range(2):
        own = current[r]
        disk = disk_ref[r].astype(F32)
        total = [disk * thrust_ref[i] for i in range(VARS)]
        for direction in range(6):
            if direction == 0:
                beside = current[0] if r == 1 else [zero] * VARS
            elif direction == 1:
                beside = current[1] if r == 0 else [zero] * VARS
            elif direction == 2:
                beside = [
                    jnp.where(sub == 0, edges[0][r][v : v + 1, :], pltpu.roll(own[v], 1, 0))
                    for v in range(VARS)
                ]
            elif direction == 3:
                beside = [
                    jnp.where(sub == 7, edges[1][r][v : v + 1, :], pltpu.roll(own[v], 7, 0))
                    for v in range(VARS)
                ]
            elif direction == 4:
                beside = [jnp.where(lane == 0, 0.0, pltpu.roll(own[v], 1, 1)) for v in range(VARS)]
            else:
                beside = [
                    jnp.where(lane == 127, 0.0, pltpu.roll(own[v], 127, 1)) for v in range(VARS)
                ]
            factor = face_ref[r, direction]
            jump = [factor * (beside[v] - own[v]) for v in range(VARS)]
            for i in range(VARS):
                for j in range(VARS):
                    total[i] = total[i] + coupling_ref[direction, i, j] * jump[j]
        residual.append(total)
        for v in range(VARS):
            current_ref[r, v] = own[v]

    def pack(k, four):
        for quarter, tile in enumerate(block_transpose(*four)):
            send_ref[pl.ds(quarter * 8 * SEND_ROWS + k, 8, stride=SEND_ROWS), :] = tile

    flow = residual[0] + residual[1] + current[0] + current[1]
    flow += [jnp.where(hit, 1.0, 0.0) for hit in fringe]
    flow += [face_ref[0, 0], face_ref[1, 1]]
    for k in range(FLOW_VALUES // 4):
        pack(k, flow[4 * k : 4 * k + 4])
    places = [(r, i, j) for r in range(2) for i in range(VARS) for j in range(VARS)]
    for k in range(25):
        four = [diag_ref[at].astype(F32) for at in places[4 * k : 4 * k + 4]]
        pack(FLOW_VALUES // 4 + k, four + [zero] * (4 - len(four)))


def from_before(x, count):
    sub, lane = sublanes(), lanes()
    if count == 4:
        return jnp.where(sub == 0, 0.0, pltpu.roll(x, 1, 0))
    width = 32 * count
    x = pltpu.roll(x, width, 1)
    return jnp.where(lane < width, jnp.where(sub == 0, 0.0, pltpu.roll(x, 1, 0)), x)


def from_after(x, count):
    sub, lane = sublanes(), lanes()
    if count == 4:
        return jnp.where(sub == 7, 0.0, pltpu.roll(x, 7, 0))
    width = 32 * count
    x = pltpu.roll(x, 128 - width, 1)
    return jnp.where(lane >= 128 - width, jnp.where(sub == 7, 0.0, pltpu.roll(x, 7, 0)), x)


def total_of(terms):
    while len(terms) > 1:
        terms = [sum(terms[at : at + 2]) for at in range(0, len(terms), 2)]
    return terms[0]


def apply(ref, vector, add=None):
    result = []
    for i in range(VARS):
        terms = [ref[i * VARS + j] * vector[j] for j in range(VARS)]
        result.append(total_of(terms + ([add[i]] if add is not None else [])))
    return result


def solve_kernel(
    moved_ref, coupling_ref, lower_ref, upper_ref, back_ref, diag, near, far, maps, moved_maps
):
    def unpack(k):
        return block_transpose(
            *[
                moved_ref[pl.ds(quarter * SEND_ROWS + k, 8, stride=4 * SEND_ROWS), :]
                for quarter in range(4)
            ]
        )

    flow = []
    for k in range(FLOW_VALUES // 4):
        flow += unpack(k)
    for k in range(25):
        for at, tile in enumerate(unpack(FLOW_VALUES // 4 + k)):
            if 4 * k + at < 98:
                diag[(4 * k + at) // 49, (4 * k + at) % 49] = tile
    residual = [flow[0:7], flow[7:14]]
    current = [flow[14:21], flow[21:28]]
    fringe = [flow[28] > 0.5, flow[29] > 0.5]
    factors = flow[30:32]
    beside = [
        [factors[0] * from_before(current[1][v], 1) for v in range(VARS)],
        [factors[1] * from_after(current[0][v], 1) for v in range(VARS)],
    ]
    for r in range(2):
        for i in range(VARS):
            for j in range(VARS):
                residual[r][i] = residual[r][i] + coupling_ref[r, i, j] * beside[r][j]
    source = [[jnp.where(fringe[r], 0.0, -residual[r][i]) for i in range(VARS)] for r in range(2)]

    def times(matrix_ref, out):
        for r in range(2):
            for i in range(VARS):
                row = [diag[r, i * VARS + j] for j in range(VARS)]
                for k in range(VARS):
                    out[r, i * VARS + k] = total_of(
                        [row[j] * matrix_ref[j, k] for j in range(VARS)]
                    )

    def multiply(a, b, out):
        for i in range(VARS):
            row = [a[i * VARS + j] for j in range(VARS)]
            for k in range(VARS):
                out[i * VARS + k] = total_of([row[j] * b[j * VARS + k] for j in range(VARS)])

    def scan(offset, shifted):
        for level, count in enumerate((1, 2)):
            a = maps.at[level]
            for at in range(49):
                moved_maps[at] = shifted(a[at], count)
            offset = apply(a, [shifted(x, count) for x in offset], offset)
            multiply(a, moved_maps, maps.at[level + 1])
        a = maps.at[2]
        x = offset
        for _ in range(7):
            x = apply(a, [shifted(part, 4) for part in x], offset)
        return x

    times(lower_ref, near)
    times(upper_ref, far)
    first = apply(diag.at[0], source[0])
    second = apply(near.at[1], first, apply(diag.at[1], source[1]))
    multiply(near.at[1], near.at[0], maps.at[0])
    second = scan(second, from_before)
    first = apply(near.at[0], [from_before(x, 1) for x in second], first)
    multiply(far.at[0], far.at[1], maps.at[0])
    update_first = scan(apply(far.at[0], second, first), from_after)
    update_second = apply(far.at[1], [from_after(x, 1) for x in update_first], second)

    results = update_first + update_second + residual[0] + residual[1]
    for k in range(BACK_ROWS):
        for quarter, tile in enumerate(block_transpose(*results[4 * k : 4 * k + 4])):
            back_ref[pl.ds(quarter * BACK_ROWS + k, 8, stride=4 * BACK_ROWS), :] = tile


def finish_kernel(returned_ref, current_ref, state_ref, residual_ref):
    results = []
    for k in range(BACK_ROWS):
        results += block_transpose(
            *[
                returned_ref[pl.ds(quarter * 8 * BACK_ROWS + k, 8, stride=BACK_ROWS), :]
                for quarter in range(4)
            ]
        )
    for r in range(2):
        for v in range(VARS):
            state_ref[r, v] = current_ref[r, v] + results[r * VARS + v]
            residual_ref[r, v] = results[14 + r * VARS + v]


VMEM = pl.BlockSpec(memory_space=pltpu.VMEM)
SMEM = pl.BlockSpec(memory_space=pltpu.SMEM)


def exchange(block, axis, parts):
    rows = block.shape[0] // parts
    if rows % 8 == 0:
        shaped = block.reshape(parts, rows, 128)
    else:
        shaped = block.reshape(block.shape[0], 1, 128)
    return lax.all_to_all(shaped, axis, 0, 0, tiled=True).reshape(block.shape)


def per_device(
    state,
    propeller,
    donor_index,
    fringe_index,
    donor_weight,
    disk_mask,
    thrust,
    face,
    coupling,
    diag_inverse,
    lower_jacobian,
    upper_jacobian,
):
    donors = pl.pallas_call(
        donor_kernel,
        out_shape=jax.ShapeDtypeStruct((GIRTHS * DONOR_ROWS, 128), F32),
        in_specs=[VMEM] * 5,
        out_specs=VMEM,
        name="donors",
    )(propeller, donor_index, fringe_index, donor_weight, state.reshape(112, 128))
    landed = exchange(donors, "girth", GIRTHS)
    send, current = pl.pallas_call(
        flow_kernel,
        out_shape=(
            jax.ShapeDtypeStruct((STREAMS * SEND_ROWS, 128), F32),
            jax.ShapeDtypeStruct(state.shape, F32),
        ),
        in_specs=[VMEM] * 5 + [SMEM] * 2,
        out_specs=(VMEM, VMEM),
        name="flow",
    )(landed, state, face, disk_mask, diag_inverse, thrust, coupling)
    moved = exchange(send, "stream", STREAMS)
    back = pl.pallas_call(
        solve_kernel,
        out_shape=jax.ShapeDtypeStruct((STREAMS * BACK_ROWS, 128), F32),
        in_specs=[VMEM] + [SMEM] * 3,
        out_specs=VMEM,
        scratch_shapes=[
            pltpu.VMEM((2, 49, 8, 128), F32),
            pltpu.VMEM((2, 49, 8, 128), F32),
            pltpu.VMEM((2, 49, 8, 128), F32),
            pltpu.VMEM((3, 49, 8, 128), F32),
            pltpu.VMEM((49, 8, 128), F32),
        ],
        name="solve",
    )(moved, coupling, lower_jacobian, upper_jacobian)
    returned = exchange(back, "stream", STREAMS)
    return pl.pallas_call(
        finish_kernel,
        out_shape=(
            jax.ShapeDtypeStruct(state.shape, F32),
            jax.ShapeDtypeStruct(state.shape, F32),
        ),
        in_specs=[VMEM] * 2,
        out_specs=(VMEM, VMEM),
        name="finish",
    )(returned, current)


def solution(mesh):
    placed = (
        P("stream", None, "girth", None),
        P(None, ("stream", "girth")),
        P(("stream", "girth"), None),
        P(("stream", "girth"), None),
        P(("stream", "girth"), None),
        P("stream", "girth", None),
        P(),
        P("stream", None, "girth", None),
        P(),
        P("stream", None, None, "girth", None),
        P(),
        P(),
    )
    return jax.shard_map(
        per_device,
        mesh=mesh,
        in_specs=placed,
        out_specs=(P("stream", None, "girth", None), P("stream", None, "girth", None)),
        check_vma=False,
    )
```

time: 372 us -> 98.7 us (0.27)
  waiting for transfers between devices: 85.6 us -> 0 us
  other arithmetic: 74.7 us -> 0 us
  local copies, waits for them, and re-layouts: 44 us -> 0 us
  matrix products: 39.8 us -> 0 us
  starting transfers between devices: 30.9 us -> 0 us
  between operations: 14.4 us -> 0.63 us
  Pallas kernels: 0 us -> 10.7 us
  blocking collectives: 76.8 us -> 86.8 us
    all_to_all x0 -> x3, blocking collectives: none -> 86.8 us  [exchange(): return lax.all_to_all(shaped, axis, 0, 0, tiled=True).reshape(block.shape)]
    all_gather x2 -> x0, waiting for transfers between devices: 81.7 us -> none  [prefix(): everything = jax.tree.map(lambda part: lax.all_gather(part, axis), shard)]
    all_gather x2 -> x0, blocking collectives: 76.8 us -> none  [prefix(): everything = jax.tree.map(lambda part: lax.all_gather(part, axis), shard)]
    dot_general x70 -> x0, other arithmetic: 65.6 us -> none  [the longest x64 65.1 us: compose(): jnp.einsum('ijc,jc->ic', later_map[0], earlier[1], precision=PRECISE)]
    dot_general x22 -> x0, matrix products: 39.8 us -> none  [the longest x4 33.3 us: advance(): compound = jnp.einsum('ijc,jkc->ikc', factor, compound, precision=PRECISE)]
    while x16 -> x0, local copies, waits for them, and re-layouts: 21.7 us -> none
    ppermute x4 -> x0, starting transfers between devices: 16.6 us -> none  [the longest x2 8.33 us: extended(): lax.ppermute(lax.slice_in_dim(block, 0, width, axis=dim), axis, backward)]
    all_to_all x2 -> x0, starting transfers between devices: 14.2 us -> none  [the longest x1 7.58 us: per_device(): lax.all_to_all(target, 'girth', split_axis=1, concat_axis=1, tiled=True)]
  transfers between devices with their start and end apart: 8 -> 0, of which waited for: 3 -> 0; matrix products, arithmetic and copies ran while one was open for 4% -> 0% of each run, Pallas kernels for 0% -> 0%
where the time goes in v1:
time: 98.7 us; the launch traced here: 98.2 us
  blocking collectives  86.8 us (88%)
  Pallas kernels  10.7 us (11%)
    all_to_all x3, blocking collectives, exchange(): return lax.all_to_all(shaped, axis, 0, 0, tiled=True).reshape(block.shape)  86.8 us
    pallas_call x1, Pallas kernels, per_device(): pl.pallas_call(solve_kernel, out_shape=jax.ShapeDtypeStruct((STREAMS * BA...  4.43 us
    pallas_call x1, Pallas kernels, per_device(): pl.pallas_call(flow_kernel, out_shape=(jax.ShapeDtypeStruct((STREAMS * SE...  2.9 us

profile of v1, /device:TPU:1, one launch (start us, length us, event | category | flops | bytes accessed | tf_op | source)
XLA Modules:
  0.0 98.2 jit_solution(918034461675212456)
XLA Ops:
  0.6 1.7 %donors.1 = f32[384,128]{1,0:T(8,128)} custom-call(f32[7,256]{1,0:T(8,128)} %prop_ref.1, s32[1,128]{1,0:T(1,128)} %index_ref.1, s32[1,128]{1,0:T(1,128)} %fringe_ref.1, f32[1,128]{1,0:T(1,128)} %weight_ref.1, f32[112,128]{1,0:T(8,128)} %bitcast.17), custom_call_target="tpu_custom_call" | custom-call | tf_op jit(solution)/shard_map/donors/pallas_call | solution.py:349
  2.3 14.9 %all_to_all.15 = f32[16,24,128]{2,1,0:T(8,128)} all-to-all(f32[16,24,128]{2,1,0:T(8,128)} %bitcast.13), channel_id=1, replica_groups=mesh['stream'=32,'girth'=16] {'girth'}, dimensions={0} | all-to-all | bytes 393216 | tf_op jit(solution)/shard_map/all_to_all | solution.py:332
  17.2 2.9 %flow.1 = (f32[1056,128]{1,0:T(8,128)}, f32[2,7,8,128]{3,2,1,0:T(8,128)}) custom-call(f32[384,128]{1,0:T(8,128)} %bitcast.12, f32[2,7,8,128]{3,2,1,0:T(8,128)} %state_ref.1, f32[2,6,8,128]{3,2,1,0:T(8,128)} %face_ref.1, s32[2,8,128]{2,1,0:T(8,128)} %disk_ref.1, bf16[2,7,7,8,128]{4,3,2,1,0:T(8,128)(2,1)} %diag_ref.1, f32[7]{0:T(128)} %thrust_ref.1, ...), custom_call_target="tpu_custom_call" | custom-call | tf_op jit(solution)/shard_map/flow/pallas_call | solution.py:357
  20.1 51.7 %all_to_all.16 = f32[1056,1,128]{2,1,0:T(1,128)} all-to-all(f32[1056,1,128]{2,1,0:T(1,128)} %bitcast.14), channel_id=1, replica_groups=mesh['stream'=32,'girth'=16] {'stream'}, dimensions={0} | all-to-all | bytes 1081344 | tf_op jit(solution)/shard_map/all_to_all | solution.py:332
  71.8 4.4 %solve.1 = f32[224,128]{1,0:T(8,128)} custom-call(f32[1056,128]{1,0:T(8,128)} %bitcast.11, f32[6,7,7]{2,1,0:T(8,128)} %coupling_ref.3, f32[7,7]{1,0:T(8,128)} %lower_ref.1, f32[7,7]{1,0:T(8,128)} %upper_ref.1), custom_call_target="tpu_custom_call" | custom-call | tf_op jit(solution)/shard_map/solve/pallas_call | solution.py:368
  76.2 20.3 %all_to_all.17 = f32[224,1,128]{2,1,0:T(1,128)} all-to-all(f32[224,1,128]{2,1,0:T(1,128)} %bitcast.16), channel_id=1, replica_groups=mesh['stream'=32,'girth'=16] {'stream'}, dimensions={0} | all-to-all | bytes 229376 | tf_op jit(solution)/shard_map/all_to_all | solution.py:332
  96.5 1.7 %finish.1 = (f32[2,7,8,128]{3,2,1,0:T(8,128)}, f32[2,7,8,128]{3,2,1,0:T(8,128)}) custom-call(f32[224,128]{1,0:T(8,128)} %bitcast.15, f32[2,7,8,128]{3,2,1,0:T(8,128)} %get-tuple-element.5.current_ref), custom_call_target="tpu_custom_call" | custom-call | tf_op jit(solution)/shard_map/finish/pallas_call | solution.py:383

commit v2 on v1

--- a/solution.py
+++ b/solution.py
@@ -351,6 +351,7 @@
         out_shape=jax.ShapeDtypeStruct((GIRTHS * DONOR_ROWS, 128), F32),
         in_specs=[VMEM] * 5,
         out_specs=VMEM,
+        compiler_params=pltpu.CompilerParams(vmem_limit_bytes=4 << 20),
         name="donors",
     )(propeller, donor_index, fringe_index, donor_weight, state.reshape(112, 128))
     landed = exchange(donors, "girth", GIRTHS)
@@ -362,6 +363,7 @@
         ),
         in_specs=[VMEM] * 5 + [SMEM] * 2,
         out_specs=(VMEM, VMEM),
+        compiler_params=pltpu.CompilerParams(vmem_limit_bytes=16 << 20),
         name="flow",
     )(landed, state, face, disk_mask, diag_inverse, thrust, coupling)
     moved = exchange(send, "stream", STREAMS)
@@ -377,6 +379,7 @@
             pltpu.VMEM((3, 49, 8, 128), F32),
             pltpu.VMEM((49, 8, 128), F32),
         ],
+        compiler_params=pltpu.CompilerParams(vmem_limit_bytes=16 << 20),
         name="solve",
     )(moved, coupling, lower_jacobian, upper_jacobian)
     returned = exchange(back, "stream", STREAMS)
@@ -388,6 +391,7 @@
         ),
         in_specs=[VMEM] * 2,
         out_specs=(VMEM, VMEM),
+        compiler_params=pltpu.CompilerParams(vmem_limit_bytes=4 << 20),
         name="finish",
     )(returned, current)
 

time: 98.7 us -> 95 us (0.963)
  Pallas kernels: 10.7 us -> 6.34 us
  local copies, waits for them, and re-layouts: 0 us -> 2.84 us
  blocking collectives: 86.8 us -> 84.8 us
    unnamed x0 -> x26, local copies, waits for them, and re-layouts: none -> 2.84 us
    all_to_all x3, blocking collectives: 86.8 us -> 84.8 us  [exchange(): return lax.all_to_all(shaped, axis, 0, 0, tiled=True).reshape(block.shape)]
    pallas_call x1, Pallas kernels: 1.72 us -> 0.16 us  [per_device(): pl.pallas_call(donor_kernel, out_shape=jax.ShapeDtypeStruct((GIRTHS * DON...]
    pallas_call x1, Pallas kernels: 2.9 us -> 1.85 us  [per_device(): pl.pallas_call(flow_kernel, out_shape=(jax.ShapeDtypeStruct((STREAMS * SE...]
where the time goes in v2:
time: 95 us; the launch traced here: 94.7 us
  blocking collectives  84.8 us (89%)
  Pallas kernels  6.34 us (7%)
  local copies, waits for them, and re-layouts  2.84 us (3%)
    all_to_all x3, blocking collectives, exchange(): return lax.all_to_all(shaped, axis, 0, 0, tiled=True).reshape(block.shape)  84.8 us
    pallas_call x1, Pallas kernels, per_device(): pl.pallas_call(solve_kernel, out_shape=jax.ShapeDtypeStruct((STREAMS * BA...  3.53 us
    unnamed x26, local copies, waits for them, and re-layouts  2.84 us

profile of v2, /device:TPU:1, one launch (start us, length us, event | category | flops | bytes accessed | tf_op | source)
XLA Modules:
  0.0 94.7 jit_solution(16691993684631083783)
XLA Ops:
  0.6 0.0 copy-start.11
  0.6 0.0 copy-start.10
  0.7 0.0 copy-start.9
  0.7 0.6 copy-done.11
  1.3 0.0 copy-done.10
  1.3 0.0 copy-done.9
  1.3 0.0 copy-start
  1.3 0.8 copy-done
  2.1 0.0 copy-start.6
  2.1 0.7 copy-done.6
  2.8 0.2 donors.1
  3.0 0.0 copy-start.2
  3.0 0.0 copy-start.1
  3.0 0.0 copy-start.3
  3.0 0.0 copy-start.4
  3.0 0.0 copy-start.5
  3.0 14.7 %all_to_all.15 = f32[16,24,128]{2,1,0:T(8,128)S(1)} all-to-all(f32[16,24,128]{2,1,0:T(8,128)S(1)} %bitcast.13), channel_id=1, replica_groups=mesh['stream'=32,'girth'=16] {'girth'}, dimensions={0} | all-to-all | bytes 393216 | tf_op jit(solution)/shard_map/all_to_all | solution.py:332
  17.8 0.0 copy-start.12
  17.8 0.0 copy-done.2
  17.8 0.0 copy-done.1
  17.8 0.0 copy-done.3
  17.8 0.0 copy-done.4
  17.8 0.0 copy-done.5
  17.8 0.6 copy-done.12
  18.4 1.8 %flow.1 = (f32[1056,128]{1,0:T(8,128)S(1)}, f32[2,7,8,128]{3,2,1,0:T(8,128)S(1)}) custom-call(f32[384,128]{1,0:T(8,128)S(1)} %bitcast.12, f32[2,7,8,128]{3,2,1,0:T(8,128)S(1)} %copy-done.1, f32[2,6,8,128]{3,2,1,0:T(8,128)S(1)} %copy-done.4, s32[2,8,128]{2,1,0:T(8,128)S(1)} %copy-done.5, bf16[2,7,7,8,128]{4,3,2,1,0:T(8,128)(2,1)S(1)} %copy-done.2, ...), custom_call_target="tpu_custom_call" | custom-call | tf_op jit(solution)/shard_map/flow/pallas_call | solution.py:358
  20.3 0.0 copy-start.7
  20.3 0.0 copy-start.8
  20.3 51.4 %all_to_all.16 = f32[1056,1,128]{2,1,0:T(1,128)S(1)} all-to-all(f32[1056,1,128]{2,1,0:T(1,128)S(1)} %bitcast.14), channel_id=1, replica_groups=mesh['stream'=32,'girth'=16] {'stream'}, dimensions={0} | all-to-all | bytes 1081344 | tf_op jit(solution)/shard_map/all_to_all | solution.py:332
  71.6 0.0 copy-done.7
  71.6 0.0 copy-done.8
  71.6 3.5 %solve.1 = f32[224,128]{1,0:T(8,128)S(1)} custom-call(f32[1056,128]{1,0:T(8,128)S(1)} %bitcast.11, f32[6,7,7]{2,1,0:T(8,128)S(1)} %copy-done.3, f32[7,7]{1,0:T(8,128)S(1)} %copy-done.7, f32[7,7]{1,0:T(8,128)S(1)} %copy-done.8), custom_call_target="tpu_custom_call" | custom-call | tf_op jit(solution)/shard_map/solve/pallas_call | solution.py:370
  75.2 18.7 %all_to_all.17 = f32[224,1,128]{2,1,0:T(1,128)S(1)} all-to-all(f32[224,1,128]{2,1,0:T(1,128)S(1)} %bitcast.16), channel_id=1, replica_groups=mesh['stream'=32,'girth'=16] {'stream'}, dimensions={0} | all-to-all | bytes 229376 | tf_op jit(solution)/shard_map/all_to_all | solution.py:332
  93.9 0.8 finish.1
Async XLA Ops:
  0.6 0.7 copy-start.11
  0.6 0.7 copy-start.10
  0.7 0.7 copy-start.9
  1.3 0.8 copy-start
  2.1 0.7 copy-start.6
  3.0 14.8 %copy-start.2 = (bf16[2,7,7,8,128]{4,3,2,1,0:T(8,128)(2,1)S(1)}, bf16[2,7,7,8,128]{4,3,2,1,0:T(8,128)(2,1)}, u32[]{:S(2)}) copy-start(bf16[2,7,7,8,128]{4,3,2,1,0:T(8,128)(2,1)} %diag_ref.1) | copy-start | bytes 602116
  3.0 14.8 %copy-start.1 = (f32[2,7,8,128]{3,2,1,0:T(8,128)S(1)}, f32[2,7,8,128]{3,2,1,0:T(8,128)}, u32[]{:S(2)}) copy-start(f32[2,7,8,128]{3,2,1,0:T(8,128)} %state_ref.1) | copy-start | bytes 172036
  3.0 14.8 %copy-start.3 = (f32[6,7,7]{2,1,0:T(8,128)S(1)}, f32[6,7,7]{2,1,0:T(8,128)}, u32[]{:S(2)}) copy-start(f32[6,7,7]{2,1,0:T(8,128)} %coupling_ref.3) | copy-start | bytes 3532
  3.0 14.7 %copy-start.4 = (f32[2,6,8,128]{3,2,1,0:T(8,128)S(1)}, f32[2,6,8,128]{3,2,1,0:T(8,128)}, u32[]{:S(2)}) copy-start(f32[2,6,8,128]{3,2,1,0:T(8,128)} %face_ref.1) | copy-start | bytes 147460
  3.0 14.7 %copy-start.5 = (s32[2,8,128]{2,1,0:T(8,128)S(1)}, s32[2,8,128]{2,1,0:T(8,128)}, u32[]{:S(2)}) copy-start(s32[2,8,128]{2,1,0:T(8,128)} %disk_ref.1) | copy-start | bytes 24580
  17.8 0.7 copy-start.12
  20.3 51.4 %copy-start.7 = (f32[7,7]{1,0:T(8,128)S(1)}, f32[7,7]{1,0:T(8,128)}, u32[]{:S(2)}) copy-start(f32[7,7]{1,0:T(8,128)} %lower_ref.1) | copy-start | bytes 592
  20.3 51.4 %copy-start.8 = (f32[7,7]{1,0:T(8,128)S(1)}, f32[7,7]{1,0:T(8,128)}, u32[]{:S(2)}) copy-start(f32[7,7]{1,0:T(8,128)} %upper_ref.1) | copy-start | bytes 592

commit v3 on v2

--- a/solution.py
+++ b/solution.py
@@ -11,9 +11,8 @@
 STREAMS = 32
 GIRTHS = 16
 DONOR_ROWS = 24
-SEND_ROWS = 33
-BACK_ROWS = 7
-FLOW_VALUES = 32
+SEND_ROWS = 32
+BACK_ROWS = 4
 
 
 def lanes(shape=(8, 128)):
@@ -42,7 +41,51 @@
     return a, b, c, d
 
 
-def donor_kernel(prop_ref, index_ref, fringe_ref, weight_ref, state_ref, out_ref):
+def pack(tiles, store):
+    for first in range(0, len(tiles) // 4, 8):
+        rows = [block_transpose(*tiles[4 * k : 4 * k + 4]) for k in range(first, first + 8)]
+        for quarter in range(4):
+            turned = jnp.swapaxes(jnp.stack([four[quarter] for four in rows]), 0, 1)
+            for g in range(8):
+                store[quarter * 8 + g, first : first + 8, :] = turned[g]
+
+
+def donor_kernel(
+    prop_hbm,
+    index_hbm,
+    fringe_hbm,
+    weight_hbm,
+    state_hbm,
+    thrust_hbm,
+    out_ref,
+    thrust_out,
+    prop_ref,
+    index_ref,
+    fringe_ref,
+    weight_ref,
+    state_ref,
+    thrust_ref,
+    sems,
+):
+    copies = [
+        pltpu.make_async_copy(source, target, sems.at[at])
+        for at, (source, target) in enumerate(
+            (
+                (index_hbm, index_ref),
+                (prop_hbm, prop_ref),
+                (weight_hbm, weight_ref),
+                (fringe_hbm, fringe_ref),
+                (state_hbm, state_ref),
+                (thrust_hbm, thrust_ref),
+            )
+        )
+    ]
+    for copy in copies:
+        copy.start()
+    for copy in copies:
+        copy.wait()
+    for v in range(VARS):
+        thrust_out[v] = jnp.full((8, 128), thrust_ref[v], F32)
     place = lax.axis_index("girth")
     index = index_ref[...]
     cells = lax.broadcasted_iota(jnp.int32, (256, 128), 0)
@@ -123,7 +166,20 @@
     coupling_ref,
     send_ref,
     current_ref,
+    down_ref,
+    up_ref,
+    partial_ref,
+    factor_ref,
+    diag_rows,
+    flow_rows,
+    sems,
 ):
+    tiles = [
+        diag_ref[r, i, j].astype(F32) for r in range(2) for i in range(VARS) for j in range(VARS)
+    ]
+    pack(tiles[2:], diag_rows)
+    diag_copy = pltpu.make_async_copy(diag_rows, send_ref.at[:, 8:, :], sems.at[0])
+    diag_copy.start()
     place = lax.axis_index("girth")
     sub, lane = sublanes(), lanes()
     sums = fringe_sums(landed_ref, place)
@@ -147,14 +203,14 @@
     zero = jnp.zeros((8, 128), F32)
     residual = []
     for r in range(2):
-        own = current[r]
         disk = disk_ref[r].astype(F32)
-        total = [disk * thrust_ref[i] for i in range(VARS)]
-        for direction in range(6):
-            if direction == 0:
-                beside = current[0] if r == 1 else [zero] * VARS
-            elif direction == 1:
-                beside = current[1] if r == 0 else [zero] * VARS
+        residual.append([disk * thrust_ref[i] for i in range(VARS)])
+    for direction in range(6):
+        jumps = []
+        for r in range(2):
+            own = current[r]
+            if direction < 2:
+                beside = [zero] * VARS if direction == r else current[1 - r]
             elif direction == 2:
                 beside = [
                     jnp.where(sub == 0, edges[0][r][v : v + 1, :], pltpu.roll(own[v], 1, 0))
@@ -172,45 +228,51 @@
                     jnp.where(lane == 127, 0.0, pltpu.roll(own[v], 127, 1)) for v in range(VARS)
                 ]
             factor = face_ref[r, direction]
-            jump = [factor * (beside[v] - own[v]) for v in range(VARS)]
-            for i in range(VARS):
-                for j in range(VARS):
-                    total[i] = total[i] + coupling_ref[direction, i, j] * jump[j]
-        residual.append(total)
+            jumps.append([factor * (beside[v] - own[v]) for v in range(VARS)])
+        for i in range(VARS):
+            for j in range(VARS):
+                weight = coupling_ref[direction, i, j]
+                for r in range(2):
+                    residual[r][i] = residual[r][i] + weight * jumps[r][j]
+    factors = [face_ref[r, r] for r in range(2)]
+    passed = []
+    for r, ref in enumerate((down_ref, up_ref)):
+        passed += [
+            total_of([coupling_ref[r, i, j] * current[1 - r][j] for j in range(VARS)])
+            for i in range(VARS)
+        ]
+        factor_ref[r] = factors[r]
         for v in range(VARS):
-            current_ref[r, v] = own[v]
-
-    def pack(k, four):
-        for quarter, tile in enumerate(block_transpose(*four)):
-            send_ref[pl.ds(quarter * 8 * SEND_ROWS + k, 8, stride=SEND_ROWS), :] = tile
-
-    flow = residual[0] + residual[1] + current[0] + current[1]
-    flow += [jnp.where(hit, 1.0, 0.0) for hit in fringe]
-    flow += [face_ref[0, 0], face_ref[1, 1]]
-    for k in range(FLOW_VALUES // 4):
-        pack(k, flow[4 * k : 4 * k + 4])
-    places = [(r, i, j) for r in range(2) for i in range(VARS) for j in range(VARS)]
-    for k in range(25):
-        four = [diag_ref[at].astype(F32) for at in places[4 * k : 4 * k + 4]]
-        pack(FLOW_VALUES // 4 + k, four + [zero] * (4 - len(four)))
+            ref[v] = passed[r * VARS + v]
+            current_ref[r, v] = current[r][v]
+            partial_ref[r, v] = residual[r][v]
+    flow = [jnp.where(fringe[r], 0.0, x) for r in range(2) for x in residual[r]]
+    flow += passed
+    flow += [jnp.where(fringe[r], 0.0, factors[r]) for r in range(2)]
+    flow += [diag_ref[0, 0, j].astype(F32) for j in range(2)]
+    pack(flow, flow_rows)
+    flow_copy = pltpu.make_async_copy(flow_rows, send_ref.at[:, :8, :], sems.at[1])
+    flow_copy.start()
+    flow_copy.wait()
+    diag_copy.wait()
 
 
 def from_before(x, count):
     sub, lane = sublanes(), lanes()
-    if count == 4:
-        return jnp.where(sub == 0, 0.0, pltpu.roll(x, 1, 0))
-    width = 32 * count
-    x = pltpu.roll(x, width, 1)
-    return jnp.where(lane < width, jnp.where(sub == 0, 0.0, pltpu.roll(x, 1, 0)), x)
+    wrapped = jnp.where(lane < 32, 0.0, pltpu.roll(x, 32, 1))
+    if count == 8:
+        return wrapped
+    return jnp.where(sub < count, pltpu.roll(wrapped, count, 0), pltpu.roll(x, count, 0))
 
 
 def from_after(x, count):
     sub, lane = sublanes(), lanes()
-    if count == 4:
-        return jnp.where(sub == 7, 0.0, pltpu.roll(x, 7, 0))
-    width = 32 * count
-    x = pltpu.roll(x, 128 - width, 1)
-    return jnp.where(lane >= 128 - width, jnp.where(sub == 7, 0.0, pltpu.roll(x, 7, 0)), x)
+    wrapped = jnp.where(lane >= 96, 0.0, pltpu.roll(x, 96, 1))
+    if count == 8:
+        return wrapped
+    return jnp.where(
+        sub >= 8 - count, pltpu.roll(wrapped, 8 - count, 0), pltpu.roll(x, 8 - count, 0)
+    )
 
 
 def total_of(terms):
@@ -228,44 +290,36 @@
 
 
 def solve_kernel(
-    moved_ref, coupling_ref, lower_ref, upper_ref, back_ref, diag, near, far, maps, moved_maps
+    moved_ref, lower_ref, upper_ref, back_ref, diag, near, far, maps, moved_maps
 ):
-    def unpack(k):
-        return block_transpose(
-            *[
-                moved_ref[pl.ds(quarter * SEND_ROWS + k, 8, stride=4 * SEND_ROWS), :]
-                for quarter in range(4)
-            ]
-        )
-
     flow = []
-    for k in range(FLOW_VALUES // 4):
-        flow += unpack(k)
-    for k in range(25):
-        for at, tile in enumerate(unpack(FLOW_VALUES // 4 + k)):
-            if 4 * k + at < 98:
-                diag[(4 * k + at) // 49, (4 * k + at) % 49] = tile
-    residual = [flow[0:7], flow[7:14]]
-    current = [flow[14:21], flow[21:28]]
-    fringe = [flow[28] > 0.5, flow[29] > 0.5]
-    factors = flow[30:32]
+    for first in range(0, SEND_ROWS, 8):
+        tiles = []
+        for quarter in range(4):
+            loaded = [moved_ref[quarter * 8 + s, first : first + 8, :] for s in range(8)]
+            tiles.append(jnp.swapaxes(jnp.stack(loaded), 0, 1))
+        for k in range(8):
+            for at, tile in enumerate(block_transpose(*[four[k] for four in tiles])):
+                place = 4 * (first + k) + at - 30
+                if place < 0:
+                    flow.append(tile)
+                else:
+                    diag[place // 49, place % 49] = tile
     beside = [
-        [factors[0] * from_before(current[1][v], 1) for v in range(VARS)],
-        [factors[1] * from_after(current[0][v], 1) for v in range(VARS)],
+        [from_before(flow[14 + v], 1) for v in range(VARS)],
+        [from_after(flow[21 + v], 1) for v in range(VARS)],
     ]
-    for r in range(2):
-        for i in range(VARS):
-            for j in range(VARS):
-                residual[r][i] = residual[r][i] + coupling_ref[r, i, j] * beside[r][j]
-    source = [[jnp.where(fringe[r], 0.0, -residual[r][i]) for i in range(VARS)] for r in range(2)]
+    source = [
+        [-flow[r * VARS + i] - flow[28 + r] * beside[r][i] for i in range(VARS)] for r in range(2)
+    ]
 
     def times(matrix_ref, out):
-        for r in range(2):
-            for i in range(VARS):
-                row = [diag[r, i * VARS + j] for j in range(VARS)]
-                for k in range(VARS):
+        for k in range(VARS):
+            column = [jnp.full((8, 128), matrix_ref[j, k], F32) for j in range(VARS)]
+            for r in range(2):
+                for i in range(VARS):
                     out[r, i * VARS + k] = total_of(
-                        [row[j] * matrix_ref[j, k] for j in range(VARS)]
+                        [diag[r, i * VARS + j] * column[j] for j in range(VARS)]
                     )
 
     def multiply(a, b, out):
@@ -275,16 +329,16 @@
                 out[i * VARS + k] = total_of([row[j] * b[j * VARS + k] for j in range(VARS)])
 
     def scan(offset, shifted):
-        for level, count in enumerate((1, 2)):
+        for level, count in enumerate((1, 2, 4)):
             a = maps.at[level]
             for at in range(49):
                 moved_maps[at] = shifted(a[at], count)
             offset = apply(a, [shifted(x, count) for x in offset], offset)
             multiply(a, moved_maps, maps.at[level + 1])
-        a = maps.at[2]
+        a = maps.at[3]
         x = offset
-        for _ in range(7):
-            x = apply(a, [shifted(part, 4) for part in x], offset)
+        for _ in range(3):
+            x = apply(a, [shifted(part, 8) for part in x], offset)
         return x
 
     times(lower_ref, near)
@@ -298,13 +352,15 @@
     update_first = scan(apply(far.at[0], second, first), from_after)
     update_second = apply(far.at[1], [from_after(x, 1) for x in update_first], second)
 
-    results = update_first + update_second + residual[0] + residual[1]
+    results = update_first + update_second + [jnp.zeros((8, 128), F32)] * 2
     for k in range(BACK_ROWS):
         for quarter, tile in enumerate(block_transpose(*results[4 * k : 4 * k + 4])):
-            back_ref[pl.ds(quarter * BACK_ROWS + k, 8, stride=4 * BACK_ROWS), :] = tile
-
-
-def finish_kernel(returned_ref, current_ref, state_ref, residual_ref):
+            back_ref[pl.ds(quarter * 8 * BACK_ROWS + k, 8, stride=BACK_ROWS), :] = tile
+
+
+def finish_kernel(
+    returned_ref, current_ref, partial_ref, factor_ref, low_ref, high_ref, state_ref, residual_ref
+):
     results = []
     for k in range(BACK_ROWS):
         results += block_transpose(
@@ -313,22 +369,20 @@
                 for quarter in range(4)
             ]
         )
-    for r in range(2):
+    for r, ref in enumerate((low_ref, high_ref)):
         for v in range(VARS):
             state_ref[r, v] = current_ref[r, v] + results[r * VARS + v]
-            residual_ref[r, v] = results[14 + r * VARS + v]
+            residual_ref[r, v] = partial_ref[r, v] + factor_ref[r] * ref[v]
 
 
 VMEM = pl.BlockSpec(memory_space=pltpu.VMEM)
 SMEM = pl.BlockSpec(memory_space=pltpu.SMEM)
+HBM = pl.BlockSpec(memory_space=pltpu.HBM)
 
 
 def exchange(block, axis, parts):
     rows = block.shape[0] // parts
-    if rows % 8 == 0:
-        shaped = block.reshape(parts, rows, 128)
-    else:
-        shaped = block.reshape(block.shape[0], 1, 128)
+    shaped = block.reshape(parts, rows, 128)
     return lax.all_to_all(shaped, axis, 0, 0, tiled=True).reshape(block.shape)
 
 
@@ -346,54 +400,80 @@
     lower_jacobian,
     upper_jacobian,
 ):
-    donors = pl.pallas_call(
+    inputs = (propeller, donor_index, fringe_index, donor_weight, state.reshape(112, 128), thrust)
+    inputs = [pltpu.with_memory_space_constraint(x, pltpu.HBM) for x in inputs]
+    donors, thrusts = pl.pallas_call(
         donor_kernel,
-        out_shape=jax.ShapeDtypeStruct((GIRTHS * DONOR_ROWS, 128), F32),
-        in_specs=[VMEM] * 5,
-        out_specs=VMEM,
+        out_shape=(
+            jax.ShapeDtypeStruct((GIRTHS * DONOR_ROWS, 128), F32),
+            jax.ShapeDtypeStruct((VARS, 8, 128), F32),
+        ),
+        in_specs=[HBM] * 6,
+        out_specs=(VMEM, VMEM),
+        scratch_shapes=[
+            pltpu.VMEM((VARS, 256), F32),
+            pltpu.VMEM((1, 128), jnp.int32),
+            pltpu.VMEM((1, 128), jnp.int32),
+            pltpu.VMEM((1, 128), F32),
+            pltpu.VMEM((112, 128), F32),
+            pltpu.SMEM((VARS,), F32),
+            pltpu.SemaphoreType.DMA((6,)),
+        ],
         compiler_params=pltpu.CompilerParams(vmem_limit_bytes=4 << 20),
         name="donors",
-    )(propeller, donor_index, fringe_index, donor_weight, state.reshape(112, 128))
+    )(*inputs)
     landed = exchange(donors, "girth", GIRTHS)
-    send, current = pl.pallas_call(
+    row = jax.ShapeDtypeStruct(state.shape[1:], F32)
+    both = jax.ShapeDtypeStruct(state.shape, F32)
+    send, current, down, up, partial, factor = pl.pallas_call(
         flow_kernel,
         out_shape=(
-            jax.ShapeDtypeStruct((STREAMS * SEND_ROWS, 128), F32),
-            jax.ShapeDtypeStruct(state.shape, F32),
+            jax.ShapeDtypeStruct((STREAMS, SEND_ROWS, 128), F32),
+            both,
+            row,
+            row,
+            both,
+            jax.ShapeDtypeStruct((2, 8, 128), F32),
         ),
-        in_specs=[VMEM] * 5 + [SMEM] * 2,
-        out_specs=(VMEM, VMEM),
+        in_specs=[VMEM] * 6 + [SMEM],
+        out_specs=(pl.BlockSpec(memory_space=pl.ANY),) + (VMEM,) * 5,
+        scratch_shapes=[
+            pltpu.VMEM((STREAMS, SEND_ROWS - 8, 128), F32),
+            pltpu.VMEM((STREAMS, 8, 128), F32),
+            pltpu.SemaphoreType.DMA((2,)),
+        ],
         compiler_params=pltpu.CompilerParams(vmem_limit_bytes=16 << 20),
         name="flow",
-    )(landed, state, face, disk_mask, diag_inverse, thrust, coupling)
-    moved = exchange(send, "stream", STREAMS)
+    )(landed, state, face, disk_mask, diag_inverse, thrusts, coupling)
+    moved = lax.all_to_all(send, "stream", 0, 0, tiled=True)
+    ahead = [(at, at + 1) for at in range(STREAMS - 1)]
+    low = lax.ppermute(down, "stream", ahead)
+    high = lax.ppermute(up, "stream", [(b, a) for a, b in ahead])
     back = pl.pallas_call(
         solve_kernel,
         out_shape=jax.ShapeDtypeStruct((STREAMS * BACK_ROWS, 128), F32),
-        in_specs=[VMEM] + [SMEM] * 3,
+        in_specs=[VMEM] + [SMEM] * 2,
         out_specs=VMEM,
         scratch_shapes=[
             pltpu.VMEM((2, 49, 8, 128), F32),
             pltpu.VMEM((2, 49, 8, 128), F32),
             pltpu.VMEM((2, 49, 8, 128), F32),
-            pltpu.VMEM((3, 49, 8, 128), F32),
+            pltpu.VMEM((4, 49, 8, 128), F32),
             pltpu.VMEM((49, 8, 128), F32),
         ],
         compiler_params=pltpu.CompilerParams(vmem_limit_bytes=16 << 20),
         name="solve",
-    )(moved, coupling, lower_jacobian, upper_jacobian)
+    )(moved, lower_jacobian, upper_jacobian)
+    back, low, high = lax.optimization_barrier((back, low, high))
     returned = exchange(back, "stream", STREAMS)
     return pl.pallas_call(
         finish_kernel,
-        out_shape=(
-            jax.ShapeDtypeStruct(state.shape, F32),
-            jax.ShapeDtypeStruct(state.shape, F32),
-        ),
-        in_specs=[VMEM] * 2,
+        out_shape=(both, both),
+        in_specs=[VMEM] * 6,
         out_specs=(VMEM, VMEM),
         compiler_params=pltpu.CompilerParams(vmem_limit_bytes=4 << 20),
         name="finish",
-    )(returned, current)
+    )(returned, current, partial, factor, low, high)
 
 
 def solution(mesh):

time: 95 us -> 91.1 us (0.959)
  blocking collectives: 84.8 us -> 31.2 us
  waiting for transfers between devices: 0 us -> 28 us
  starting transfers between devices: 0 us -> 22.8 us
  local copies, waits for them, and re-layouts: 2.84 us -> 0.04 us
  Pallas kernels: 6.34 us -> 7.8 us
    all_to_all x3 -> x2, blocking collectives: 84.8 us -> 31.2 us  [exchange(): return lax.all_to_all(shaped, axis, 0, 0, tiled=True).reshape(block.shape)]
    all_to_all x0 -> x1, waiting for transfers between devices: none -> 28 us  [per_device(): moved = lax.all_to_all(send, 'stream', 0, 0, tiled=True)]
    all_to_all x0 -> x1, starting transfers between devices: none -> 17.4 us  [per_device(): moved = lax.all_to_all(send, 'stream', 0, 0, tiled=True)]
    ppermute x0 -> x2, starting transfers between devices: none -> 5.46 us  [the longest x1 3.54 us: per_device(): low = lax.ppermute(down, 'stream', ahead)]
    unnamed x26 -> x14, local copies, waits for them, and re-layouts: 2.84 us -> 0.04 us
    pallas_call x3, Pallas kernels: 2.8 us -> 4.81 us  [the longest x1 2.92 us: per_device(): pl.pallas_call(flow_kernel, out_shape=(jax.ShapeDtypeStruct((STREAMS, SEN...]
  transfers between devices with their start and end apart: 0 -> 3, of which waited for: 0 -> 1; matrix products, arithmetic and copies ran while one was open for 0% -> 0% of each run, Pallas kernels for 0% -> 3%
where the time goes in v3:
time: 91.1 us; the launch traced here: 90.7 us
  blocking collectives  31.2 us (34%)
  waiting for transfers between devices  28 us (31%)
  starting transfers between devices  22.8 us (25%)
  Pallas kernels  7.8 us (9%)
    all_to_all x2, blocking collectives, exchange(): return lax.all_to_all(shaped, axis, 0, 0, tiled=True).reshape(block.shape)  31.2 us
    all_to_all x1, waiting for transfers between devices, per_device(): moved = lax.all_to_all(send, 'stream', 0, 0, tiled=True)  28 us
    all_to_all x1, starting transfers between devices, per_device(): moved = lax.all_to_all(send, 'stream', 0, 0, tiled=True)  17.4 us
    ppermute x1, starting transfers between devices, per_device(): low = lax.ppermute(down, 'stream', ahead)  3.54 us
    pallas_call x1, Pallas kernels, per_device(): pl.pallas_call(solve_kernel, out_shape=jax.ShapeDtypeStruct((STREAMS * BA...  3 us
    pallas_call x1, Pallas kernels, per_device(): pl.pallas_call(flow_kernel, out_shape=(jax.ShapeDtypeStruct((STREAMS, SEN...  2.92 us
    ppermute x1, starting transfers between devices, per_device(): high = lax.ppermute(up, 'stream', [(b, a) for a, b in ahead])  1.92 us
  transfers between devices with their start and end apart: 3, of which 1 were waited for; matrix products, arithmetic and copies ran while one was open for 0% of the time, Pallas kernels for 3%

profile of v3, /device:TPU:1, one launch (start us, length us, event | category | flops | bytes accessed | tf_op | source)
XLA Modules:
  0.0 90.7 jit_solution(145969325258795675)
XLA Ops:
  0.6 1.1 %donors.1 = (f32[384,128]{1,0:T(8,128)S(1)}, f32[7,8,128]{2,1,0:T(8,128)S(1)}) custom-call(f32[7,256]{1,0:T(8,128)} %prop_hbm.1, s32[1,128]{1,0:T(1,128)} %index_hbm.1, s32[1,128]{1,0:T(1,128)} %fringe_hbm.1, f32[1,128]{1,0:T(1,128)} %weight_hbm.1, f32[112,128]{1,0:T(8,128)} %bitcast.8, f32[7]{0:T(128)} %thrust_hbm.1), custom_call_target="tpu_custom_call" | custom-call | tf_op jit(solution)/shard_map/donors/pallas_call | solution.py:405
  1.7 0.0 copy-start.1
  1.8 0.0 copy-start
  1.8 0.0 copy-start.2
  1.8 0.0 copy-start.3
  1.8 0.0 copy-start.4
  1.8 14.7 %all_to_all.15 = f32[16,24,128]{2,1,0:T(8,128)S(1)} all-to-all(f32[16,24,128]{2,1,0:T(8,128)S(1)} %bitcast.9), channel_id=1, replica_groups=mesh['stream'=32,'girth'=16] {'girth'}, dimensions={0} | all-to-all | bytes 393216 | tf_op jit(solution)/shard_map/all_to_all | solution.py:386
  16.5 0.0 copy-done.1
  16.5 0.0 copy-done
  16.5 0.0 copy-done.2
  16.5 0.0 copy-done.3
  16.5 0.0 copy-done.4
  16.5 2.9 %flow.1 = (f32[32,32,128]{2,1,0:T(8,128)}, f32[2,7,8,128]{3,2,1,0:T(8,128)S(1)}, f32[7,8,128]{2,1,0:T(8,128)S(1)}, f32[7,8,128]{2,1,0:T(8,128)S(1)}, f32[2,7,8,1...) custom-call(f32[384,128]{1,0:T(8,128)S(1)} %bitcast.5, f32[2,7,8,128]{3,2,1,0:T(8,128)S(1)} %copy-done, ...), custom_call_target="tpu_custom_call" | custom-call | tf_op jit(solution)/shard_map/flow/pallas_call | solution.py:428
  19.5 0.0 copy-start.5
  19.5 0.0 copy-start.6
  19.5 17.4 %all-to-all-start.1 = ((f32[32,32,128]{2,1,0:T(8,128)}), f32[32,32,128]{2,1,0:T(8,128)S(1)}, u32[]{:S(2)}, u32[]{:S(2)}) async-start(f32[32,32,128]{2,1,0:T(8,128)} %get-tuple-element.15), calls=%async_computation.1 | async-start | bytes 1048576 | tf_op jit(solution)/shard_map/all_to_all | solution.py:448
  36.9 3.5 %collective-permute-start = (f32[7,8,128]{2,1,0:T(8,128)S(1)}, f32[7,8,128]{2,1,0:T(8,128)S(1)}, u32[]{:S(2)}, u32[]{:S(2)}) collective-permute-start(f32[7,8,128]{2,1,0:T(8,128)S(1)} %get-tuple-element.16), channel_id=1, source_target_pairs={{0,16},{16,32},{32,48},{48,64},{64,80},{80,96},{96,112},{112,128},... | collective-permute-start | bytes 86024 | tf_op jit(solution)/shard_map/ppermute | solution.py:450
  40.4 1.9 %collective-permute-start.1 = (f32[7,8,128]{2,1,0:T(8,128)S(1)}, f32[7,8,128]{2,1,0:T(8,128)S(1)}, u32[]{:S(2)}, u32[]{:S(2)}) collective-permute-start(f32[7,8,128]{2,1,0:T(8,128)S(1)} %get-tuple-element.17), channel_id=1, source_target_pairs={{16,0},{32,16},{48,32},{64,48},{80,64},{96,80},{112,96},{128,112},... | collective-permute-start | bytes 86024 | tf_op jit(solution)/shard_map/ppermute | solution.py:451
  42.3 28.0 %all-to-all-done.1.moved_ref = f32[32,32,128]{2,1,0:T(8,128)S(1)} async-done(((f32[32,32,128]{2,1,0:T(8,128)}), f32[32,32,128]{2,1,0:T(8,128)S(1)}, u32[]{:S(2)}, u32[]{:S(2)}) %all-to-all-start.1) | async-done | bytes 524320 | tf_op jit(solution)/shard_map/all_to_all | solution.py:448
  70.4 0.0 copy-done.5
  70.4 0.0 copy-done.6
  70.4 3.0 %solve.1 = f32[128,128]{1,0:T(8,128)S(1)} custom-call(f32[32,32,128]{2,1,0:T(8,128)S(1)} %all-to-all-done.1.moved_ref, f32[7,7]{1,0:T(8,128)S(1)} %copy-done.5, f32[7,7]{1,0:T(8,128)S(1)} %copy-done.6), custom_call_target="tpu_custom_call" | custom-call | tf_op jit(solution)/shard_map/solve/pallas_call | solution.py:452
  73.4 0.0 collective-permute-done.low_ref
  73.4 0.0 collective-permute-done.1.high_ref
  73.4 16.5 %all_to_all.16 = f32[32,4,128]{2,1,0:T(4,128)S(1)} all-to-all(f32[32,4,128]{2,1,0:T(4,128)S(1)} %bitcast.6), channel_id=1, replica_groups=mesh['stream'=32,'girth'=16] {'stream'}, dimensions={0} | all-to-all | bytes 131072 | tf_op jit(solution)/shard_map/all_to_all | solution.py:386
  89.9 0.8 finish.1
Async XLA Ops:
  1.7 14.8 %copy-start.1 = (bf16[2,7,7,8,128]{4,3,2,1,0:T(8,128)(2,1)S(1)}, bf16[2,7,7,8,128]{4,3,2,1,0:T(8,128)(2,1)}, u32[]{:S(2)}) copy-start(bf16[2,7,7,8,128]{4,3,2,1,0:T(8,128)(2,1)} %diag_ref.1) | copy-start | bytes 602116
  1.8 14.8 %copy-start = (f32[2,7,8,128]{3,2,1,0:T(8,128)S(1)}, f32[2,7,8,128]{3,2,1,0:T(8,128)}, u32[]{:S(2)}) copy-start(f32[2,7,8,128]{3,2,1,0:T(8,128)} %state_ref.1) | copy-start | bytes 172036
  1.8 14.8 %copy-start.2 = (f32[2,6,8,128]{3,2,1,0:T(8,128)S(1)}, f32[2,6,8,128]{3,2,1,0:T(8,128)}, u32[]{:S(2)}) copy-start(f32[2,6,8,128]{3,2,1,0:T(8,128)} %face_ref.1) | copy-start | bytes 147460
  1.8 14.7 %copy-start.3 = (f32[6,7,7]{2,1,0:T(8,128)S(1)}, f32[6,7,7]{2,1,0:T(8,128)}, u32[]{:S(2)}) copy-start(f32[6,7,7]{2,1,0:T(8,128)} %coupling_ref.1) | copy-start | bytes 3532
  1.8 14.7 %copy-start.4 = (s32[2,8,128]{2,1,0:T(8,128)S(1)}, s32[2,8,128]{2,1,0:T(8,128)}, u32[]{:S(2)}) copy-start(s32[2,8,128]{2,1,0:T(8,128)} %disk_ref.1) | copy-start | bytes 24580
  19.5 50.9 %copy-start.5 = (f32[7,7]{1,0:T(8,128)S(1)}, f32[7,7]{1,0:T(8,128)}, u32[]{:S(2)}) copy-start(f32[7,7]{1,0:T(8,128)} %lower_ref.1) | copy-start | bytes 592
  19.5 50.9 %copy-start.6 = (f32[7,7]{1,0:T(8,128)S(1)}, f32[7,7]{1,0:T(8,128)}, u32[]{:S(2)}) copy-start(f32[7,7]{1,0:T(8,128)} %upper_ref.1) | copy-start | bytes 592
  19.5 50.9 %all-to-all-start.1 = ((f32[32,32,128]{2,1,0:T(8,128)}), f32[32,32,128]{2,1,0:T(8,128)S(1)}, u32[]{:S(2)}, u32[]{:S(2)}) async-start(f32[32,32,128]{2,1,0:T(8,128)} %get-tuple-element.15), calls=%async_computation.1 | async-start | bytes 1048576 | tf_op jit(solution)/shard_map/all_to_all | solution.py:448
  36.9 36.5 %collective-permute-start = (f32[7,8,128]{2,1,0:T(8,128)S(1)}, f32[7,8,128]{2,1,0:T(8,128)S(1)}, u32[]{:S(2)}, u32[]{:S(2)}) collective-permute-start(f32[7,8,128]{2,1,0:T(8,128)S(1)} %get-tuple-element.16), channel_id=1, source_target_pairs={{0,16},{16,32},{32,48},{48,64},{64,80},{80,96},{96,112},{112,128},... | collective-permute-start | bytes 86024 | tf_op jit(solution)/shard_map/ppermute | solution.py:450
  40.4 33.0 %collective-permute-start.1 = (f32[7,8,128]{2,1,0:T(8,128)S(1)}, f32[7,8,128]{2,1,0:T(8,128)S(1)}, u32[]{:S(2)}, u32[]{:S(2)}) collective-permute-start(f32[7,8,128]{2,1,0:T(8,128)S(1)} %get-tuple-element.17), channel_id=1, source_target_pairs={{16,0},{32,16},{48,32},{64,48},{80,64},{96,80},{112,96},{128,112},... | collective-permute-start | bytes 86024 | tf_op jit(solution)/shard_map/ppermute | solution.py:451

commit v4 on v3

--- a/solution.py
+++ b/solution.py
@@ -41,13 +41,13 @@
     return a, b, c, d
 
 
-def pack(tiles, store):
+def pack(tiles, store, base):
     for first in range(0, len(tiles) // 4, 8):
         rows = [block_transpose(*tiles[4 * k : 4 * k + 4]) for k in range(first, first + 8)]
         for quarter in range(4):
             turned = jnp.swapaxes(jnp.stack([four[quarter] for four in rows]), 0, 1)
             for g in range(8):
-                store[quarter * 8 + g, first : first + 8, :] = turned[g]
+                store[quarter * 8 + g, base + first : base + first + 8, :] = turned[g]
 
 
 def donor_kernel(
@@ -163,23 +163,22 @@
     disk_ref,
     diag_ref,
     thrust_ref,
-    coupling_ref,
+    coupling_hbm,
     send_ref,
     current_ref,
     down_ref,
     up_ref,
     partial_ref,
     factor_ref,
-    diag_rows,
-    flow_rows,
-    sems,
+    coupling_ref,
+    sem,
 ):
+    coupling_copy = pltpu.make_async_copy(coupling_hbm, coupling_ref, sem)
+    coupling_copy.start()
     tiles = [
         diag_ref[r, i, j].astype(F32) for r in range(2) for i in range(VARS) for j in range(VARS)
     ]
-    pack(tiles[2:], diag_rows)
-    diag_copy = pltpu.make_async_copy(diag_rows, send_ref.at[:, 8:, :], sems.at[0])
-    diag_copy.start()
+    pack(tiles[2:], send_ref, 8)
     place = lax.axis_index("girth")
     sub, lane = sublanes(), lanes()
     sums = fringe_sums(landed_ref, place)
@@ -205,6 +204,7 @@
     for r in range(2):
         disk = disk_ref[r].astype(F32)
         residual.append([disk * thrust_ref[i] for i in range(VARS)])
+    coupling_copy.wait()
     for direction in range(6):
         jumps = []
         for r in range(2):
@@ -250,11 +250,7 @@
     flow += passed
     flow += [jnp.where(fringe[r], 0.0, factors[r]) for r in range(2)]
     flow += [diag_ref[0, 0, j].astype(F32) for j in range(2)]
-    pack(flow, flow_rows)
-    flow_copy = pltpu.make_async_copy(flow_rows, send_ref.at[:, :8, :], sems.at[1])
-    flow_copy.start()
-    flow_copy.wait()
-    diag_copy.wait()
+    pack(flow, send_ref, 0)
 
 
 def from_before(x, count):
@@ -289,8 +285,15 @@
     return result
 
 
+def spread_kernel(lower_ref, upper_ref, out_ref):
+    for which, ref in enumerate((lower_ref, upper_ref)):
+        for i in range(VARS):
+            for j in range(VARS):
+                out_ref[which, i * VARS + j] = jnp.full((8, 128), ref[i, j], F32)
+
+
 def solve_kernel(
-    moved_ref, lower_ref, upper_ref, back_ref, diag, near, far, maps, moved_maps
+    moved_ref, spread_ref, back_ref, diag, near, far, maps, moved_maps
 ):
     flow = []
     for first in range(0, SEND_ROWS, 8):
@@ -313,9 +316,9 @@
         [-flow[r * VARS + i] - flow[28 + r] * beside[r][i] for i in range(VARS)] for r in range(2)
     ]
 
-    def times(matrix_ref, out):
+    def times(which, out):
         for k in range(VARS):
-            column = [jnp.full((8, 128), matrix_ref[j, k], F32) for j in range(VARS)]
+            column = [spread_ref[which, j * VARS + k] for j in range(VARS)]
             for r in range(2):
                 for i in range(VARS):
                     out[r, i * VARS + k] = total_of(
@@ -341,8 +344,8 @@
             x = apply(a, [shifted(part, 8) for part in x], offset)
         return x
 
-    times(lower_ref, near)
-    times(upper_ref, far)
+    times(0, near)
+    times(1, far)
     first = apply(diag.at[0], source[0])
     second = apply(near.at[1], first, apply(diag.at[1], source[1]))
     multiply(near.at[1], near.at[0], maps.at[0])
@@ -435,13 +438,9 @@
             both,
             jax.ShapeDtypeStruct((2, 8, 128), F32),
         ),
-        in_specs=[VMEM] * 6 + [SMEM],
-        out_specs=(pl.BlockSpec(memory_space=pl.ANY),) + (VMEM,) * 5,
-        scratch_shapes=[
-            pltpu.VMEM((STREAMS, SEND_ROWS - 8, 128), F32),
-            pltpu.VMEM((STREAMS, 8, 128), F32),
-            pltpu.SemaphoreType.DMA((2,)),
-        ],
+        in_specs=[VMEM] * 6 + [pl.BlockSpec(memory_space=pl.ANY)],
+        out_specs=(VMEM,) * 6,
+        scratch_shapes=[pltpu.SMEM((6, VARS, VARS), F32), pltpu.SemaphoreType.DMA(())],
         compiler_params=pltpu.CompilerParams(vmem_limit_bytes=16 << 20),
         name="flow",
     )(landed, state, face, disk_mask, diag_inverse, thrusts, coupling)
@@ -449,10 +448,19 @@
     ahead = [(at, at + 1) for at in range(STREAMS - 1)]
     low = lax.ppermute(down, "stream", ahead)
     high = lax.ppermute(up, "stream", [(b, a) for a, b in ahead])
+    lower, upper, _ = lax.optimization_barrier((lower_jacobian, upper_jacobian, factor))
+    spread = pl.pallas_call(
+        spread_kernel,
+        out_shape=jax.ShapeDtypeStruct((2, VARS * VARS, 8, 128), F32),
+        in_specs=[SMEM] * 2,
+        out_specs=VMEM,
+        compiler_params=pltpu.CompilerParams(vmem_limit_bytes=4 << 20),
+        name="spread",
+    )(lower, upper)
     back = pl.pallas_call(
         solve_kernel,
         out_shape=jax.ShapeDtypeStruct((STREAMS * BACK_ROWS, 128), F32),
-        in_specs=[VMEM] + [SMEM] * 2,
+        in_specs=[VMEM] * 2,
         out_specs=VMEM,
         scratch_shapes=[
             pltpu.VMEM((2, 49, 8, 128), F32),
@@ -463,7 +471,7 @@
         ],
         compiler_params=pltpu.CompilerParams(vmem_limit_bytes=16 << 20),
         name="solve",
-    )(moved, lower_jacobian, upper_jacobian)
+    )(moved, spread)
     back, low, high = lax.optimization_barrier((back, low, high))
     returned = exchange(back, "stream", STREAMS)
     return pl.pallas_call(

time: 91.1 us -> 89.7 us (0.985)
  no operation moved by 1% of the time
where the time goes in v4:
time: 89.7 us; the launch traced here: 89.3 us
  blocking collectives  31.2 us (35%)
  waiting for transfers between devices  27.3 us (30%)
  starting transfers between devices  22.8 us (25%)
  Pallas kernels  7.09 us (8%)
    all_to_all x2, blocking collectives, exchange(): return lax.all_to_all(shaped, axis, 0, 0, tiled=True).reshape(block.shape)  31.2 us
    all_to_all x1, waiting for transfers between devices, per_device(): moved = lax.all_to_all(send, 'stream', 0, 0, tiled=True)  27.3 us
    all_to_all x1, starting transfers between devices, per_device(): moved = lax.all_to_all(send, 'stream', 0, 0, tiled=True)  17.4 us
    ppermute x1, starting transfers between devices, per_device(): low = lax.ppermute(down, 'stream', ahead)  3.54 us
    pallas_call x1, Pallas kernels, per_device(): pl.pallas_call(solve_kernel, out_shape=jax.ShapeDtypeStruct((STREAMS * BA...  2.35 us
    pallas_call x1, Pallas kernels, per_device(): pl.pallas_call(flow_kernel, out_shape=(jax.ShapeDtypeStruct((STREAMS, SEN...  2.16 us
    ppermute x1, starting transfers between devices, per_device(): high = lax.ppermute(up, 'stream', [(b, a) for a, b in ahead])  1.92 us
  transfers between devices with their start and end apart: 3, of which 1 were waited for; matrix products, arithmetic and copies ran while one was open for 0% of the time, Pallas kernels for 3%

profile of v4, /device:TPU:1, one launch (start us, length us, event | category | flops | bytes accessed | tf_op | source)
XLA Modules:
  0.0 89.3 jit_solution(15168176754535492930)
XLA Ops:
  0.6 1.1 %donors.1 = (f32[384,128]{1,0:T(8,128)S(1)}, f32[7,8,128]{2,1,0:T(8,128)S(1)}) custom-call(f32[7,256]{1,0:T(8,128)} %prop_hbm.1, s32[1,128]{1,0:T(1,128)} %index_hbm.1, s32[1,128]{1,0:T(1,128)} %fringe_hbm.1, f32[1,128]{1,0:T(1,128)} %weight_hbm.1, f32[112,128]{1,0:T(8,128)} %bitcast.8, f32[7]{0:T(128)} %thrust_hbm.1), custom_call_target="tpu_custom_call" | custom-call | tf_op jit(solution)/shard_map/donors/pallas_call | solution.py:408
  1.7 0.0 copy-start.1
  1.8 0.0 copy-start
  1.8 0.0 copy-start.2
  1.8 0.0 copy-start.3
  1.8 0.0 copy-start.4
  1.8 14.7 %all_to_all.15 = f32[16,24,128]{2,1,0:T(8,128)S(1)} all-to-all(f32[16,24,128]{2,1,0:T(8,128)S(1)} %bitcast.9), channel_id=1, replica_groups=mesh['stream'=32,'girth'=16] {'girth'}, dimensions={0} | all-to-all | bytes 393216 | tf_op jit(solution)/shard_map/all_to_all | solution.py:389
  16.5 0.0 copy-done.1
  16.5 0.0 copy-done
  16.5 0.0 copy-done.2
  16.5 0.0 copy-done.3
  16.5 0.0 copy-done.4
  16.5 2.2 %flow.1 = (f32[32,32,128]{2,1,0:T(8,128)}, f32[2,7,8,128]{3,2,1,0:T(8,128)S(1)}, f32[7,8,128]{2,1,0:T(8,128)S(1)}, f32[7,8,128]{2,1,0:T(8,128)S(1)}, f32[2,7,8,1...) custom-call(f32[384,128]{1,0:T(8,128)S(1)} %bitcast.5, f32[2,7,8,128]{3,2,1,0:T(8,128)S(1)} %copy-done, ...), custom_call_target="tpu_custom_call" | custom-call | tf_op jit(solution)/shard_map/flow/pallas_call | solution.py:431
  18.7 0.0 copy-start.6
  18.7 17.4 %all-to-all-start.1 = ((f32[32,32,128]{2,1,0:T(8,128)}), f32[32,32,128]{2,1,0:T(8,128)S(1)}, u32[]{:S(2)}, u32[]{:S(2)}) async-start(f32[32,32,128]{2,1,0:T(8,128)} %get-tuple-element.17), calls=%async_computation.1 | async-start | bytes 1048576 | tf_op jit(solution)/shard_map/all_to_all | solution.py:447
  36.1 0.0 copy-start.5
  36.1 3.5 %collective-permute-start = (f32[7,8,128]{2,1,0:T(8,128)S(1)}, f32[7,8,128]{2,1,0:T(8,128)S(1)}, u32[]{:S(2)}, u32[]{:S(2)}) collective-permute-start(f32[7,8,128]{2,1,0:T(8,128)S(1)} %get-tuple-element.21), channel_id=1, source_target_pairs={{0,16},{16,32},{32,48},{48,64},{64,80},{80,96},{96,112},{112,128},... | collective-permute-start | bytes 86024 | tf_op jit(solution)/shard_map/ppermute | solution.py:449
  39.7 1.9 %collective-permute-start.1 = (f32[7,8,128]{2,1,0:T(8,128)S(1)}, f32[7,8,128]{2,1,0:T(8,128)S(1)}, u32[]{:S(2)}, u32[]{:S(2)}) collective-permute-start(f32[7,8,128]{2,1,0:T(8,128)S(1)} %get-tuple-element.22), channel_id=1, source_target_pairs={{16,0},{32,16},{48,32},{64,48},{80,64},{96,80},{112,96},{128,112},... | collective-permute-start | bytes 86024 | tf_op jit(solution)/shard_map/ppermute | solution.py:450
  41.6 0.0 copy-done.6
  41.6 0.0 copy-done.5
  41.6 0.7 spread.1.spread_ref
  42.3 27.3 %all-to-all-done.1.moved_ref = f32[32,32,128]{2,1,0:T(8,128)S(1)} async-done(((f32[32,32,128]{2,1,0:T(8,128)}), f32[32,32,128]{2,1,0:T(8,128)S(1)}, u32[]{:S(2)}, u32[]{:S(2)}) %all-to-all-start.1) | async-done | bytes 524320 | tf_op jit(solution)/shard_map/all_to_all | solution.py:447
  69.6 2.3 %solve.1 = f32[128,128]{1,0:T(8,128)S(1)} custom-call(f32[32,32,128]{2,1,0:T(8,128)S(1)} %all-to-all-done.1.moved_ref, f32[2,49,8,128]{3,2,1,0:T(8,128)S(1)} %spread.1.spread_ref), custom_call_target="tpu_custom_call" | custom-call | tf_op jit(solution)/shard_map/solve/pallas_call | solution.py:460
  72.0 0.0 collective-permute-done.low_ref
  72.0 0.0 collective-permute-done.1.high_ref
  72.0 16.5 %all_to_all.16 = f32[32,4,128]{2,1,0:T(4,128)S(1)} all-to-all(f32[32,4,128]{2,1,0:T(4,128)S(1)} %bitcast.7), channel_id=1, replica_groups=mesh['stream'=32,'girth'=16] {'stream'}, dimensions={0} | all-to-all | bytes 131072 | tf_op jit(solution)/shard_map/all_to_all | solution.py:389
  88.5 0.8 finish.1
Async XLA Ops:
  1.7 14.8 %copy-start.1 = (bf16[2,7,7,8,128]{4,3,2,1,0:T(8,128)(2,1)S(1)}, bf16[2,7,7,8,128]{4,3,2,1,0:T(8,128)(2,1)}, u32[]{:S(2)}) copy-start(bf16[2,7,7,8,128]{4,3,2,1,0:T(8,128)(2,1)} %diag_ref.1) | copy-start | bytes 602116
  1.8 14.8 %copy-start = (f32[2,7,8,128]{3,2,1,0:T(8,128)S(1)}, f32[2,7,8,128]{3,2,1,0:T(8,128)}, u32[]{:S(2)}) copy-start(f32[2,7,8,128]{3,2,1,0:T(8,128)} %state_ref.1) | copy-start | bytes 172036
  1.8 14.8 %copy-start.2 = (f32[2,6,8,128]{3,2,1,0:T(8,128)S(1)}, f32[2,6,8,128]{3,2,1,0:T(8,128)}, u32[]{:S(2)}) copy-start(f32[2,6,8,128]{3,2,1,0:T(8,128)} %face_ref.1) | copy-start | bytes 147460
  1.8 14.7 %copy-start.3 = (f32[6,7,7]{2,1,0:T(8,128)S(1)}, f32[6,7,7]{2,1,0:T(8,128)}, u32[]{:S(2)}) copy-start(f32[6,7,7]{2,1,0:T(8,128)} %coupling_hbm.1) | copy-start | bytes 3532
  1.8 14.7 %copy-start.4 = (s32[2,8,128]{2,1,0:T(8,128)S(1)}, s32[2,8,128]{2,1,0:T(8,128)}, u32[]{:S(2)}) copy-start(s32[2,8,128]{2,1,0:T(8,128)} %disk_ref.1) | copy-start | bytes 24580
  18.7 22.9 %copy-start.6 = (f32[7,7]{1,0:T(8,128)S(1)}, f32[7,7]{1,0:T(8,128)}, u32[]{:S(2)}) copy-start(f32[7,7]{1,0:T(8,128)} %upper_ref) | copy-start | bytes 592
  18.7 50.9 %all-to-all-start.1 = ((f32[32,32,128]{2,1,0:T(8,128)}), f32[32,32,128]{2,1,0:T(8,128)S(1)}, u32[]{:S(2)}, u32[]{:S(2)}) async-start(f32[32,32,128]{2,1,0:T(8,128)} %get-tuple-element.17), calls=%async_computation.1 | async-start | bytes 1048576 | tf_op jit(solution)/shard_map/all_to_all | solution.py:447
  36.1 5.5 %copy-start.5 = (f32[7,7]{1,0:T(8,128)S(1)}, f32[7,7]{1,0:T(8,128)}, u32[]{:S(2)}) copy-start(f32[7,7]{1,0:T(8,128)} %lower_ref) | copy-start | bytes 592
  36.1 35.8 %collective-permute-start = (f32[7,8,128]{2,1,0:T(8,128)S(1)}, f32[7,8,128]{2,1,0:T(8,128)S(1)}, u32[]{:S(2)}, u32[]{:S(2)}) collective-permute-start(f32[7,8,128]{2,1,0:T(8,128)S(1)} %get-tuple-element.21), channel_id=1, source_target_pairs={{0,16},{16,32},{32,48},{48,64},{64,80},{80,96},{96,112},{112,128},... | collective-permute-start | bytes 86024 | tf_op jit(solution)/shard_map/ppermute | solution.py:449
  39.7 32.3 %collective-permute-start.1 = (f32[7,8,128]{2,1,0:T(8,128)S(1)}, f32[7,8,128]{2,1,0:T(8,128)S(1)}, u32[]{:S(2)}, u32[]{:S(2)}) collective-permute-start(f32[7,8,128]{2,1,0:T(8,128)S(1)} %get-tuple-element.22), channel_id=1, source_target_pairs={{16,0},{32,16},{48,32},{64,48},{80,64},{96,80},{112,96},{128,112},... | collective-permute-start | bytes 86024 | tf_op jit(solution)/shard_map/ppermute | solution.py:450

commit v5 on v4

--- a/solution.py
+++ b/solution.py
@@ -82,17 +82,17 @@
     ]
     for copy in copies:
         copy.start()
-    for copy in copies:
+    place = lax.axis_index("girth")
+    for copy in copies[:2]:
         copy.wait()
-    for v in range(VARS):
-        thrust_out[v] = jnp.full((8, 128), thrust_ref[v], F32)
-    place = lax.axis_index("girth")
     index = index_ref[...]
     cells = lax.broadcasted_iota(jnp.int32, (256, 128), 0)
     pick = jnp.where(cells == index, 1.0, 0.0).astype(BF16)
     values = jnp.zeros((VARS, 128), F32)
     for part in split_parts(prop_ref[...]):
         values = values + jnp.dot(part.astype(BF16), pick, preferred_element_type=F32)
+    for copy in copies[2:]:
+        copy.wait()
     values = values * weight_ref[...]
     target = jnp.where(index >= 0, fringe_ref[...], -1).astype(F32)
     edges = [
@@ -102,6 +102,8 @@
         )
         for row in range(2)
     ]
+    for v in range(VARS):
+        thrust_out[v] = jnp.full((8, 128), thrust_ref[v], F32)
     upper = lax.rem(place + 1, GIRTHS)
     for peer in range(GIRTHS):
         start = peer * DONOR_ROWS
@@ -253,28 +255,41 @@
     pack(flow, send_ref, 0)
 
 
-def from_before(x, count):
+def from_before(x):
     sub, lane = sublanes(), lanes()
     wrapped = jnp.where(lane < 32, 0.0, pltpu.roll(x, 32, 1))
-    if count == 8:
-        return wrapped
-    return jnp.where(sub < count, pltpu.roll(wrapped, count, 0), pltpu.roll(x, count, 0))
-
-
-def from_after(x, count):
+    return jnp.where(sub < 1, pltpu.roll(wrapped, 1, 0), pltpu.roll(x, 1, 0))
+
+
+def from_after(x):
     sub, lane = sublanes(), lanes()
     wrapped = jnp.where(lane >= 96, 0.0, pltpu.roll(x, 96, 1))
-    if count == 8:
-        return wrapped
-    return jnp.where(
-        sub >= 8 - count, pltpu.roll(wrapped, 8 - count, 0), pltpu.roll(x, 8 - count, 0)
-    )
+    return jnp.where(sub >= 7, pltpu.roll(wrapped, 7, 0), pltpu.roll(x, 7, 0))
+
+
+def within_before(x, count, fill=0.0):
+    return jnp.where(sublanes() < count, fill, pltpu.roll(x, count, 0))
+
+
+def within_after(x, count, fill=0.0):
+    return jnp.where(sublanes() >= 8 - count, fill, pltpu.roll(x, 8 - count, 0))
+
+
+def eight_before(x):
+    x = jnp.where(lanes() < 32, 0.0, pltpu.roll(x, 32, 1))
+    return jnp.broadcast_to(x[7:8, :], (8, 128))
+
+
+def eight_after(x):
+    x = jnp.where(lanes() >= 96, 0.0, pltpu.roll(x, 96, 1))
+    return jnp.broadcast_to(x[0:1, :], (8, 128))
 
 
 def total_of(terms):
-    while len(terms) > 1:
-        terms = [sum(terms[at : at + 2]) for at in range(0, len(terms), 2)]
-    return terms[0]
+    total = terms[0]
+    for term in terms[1:]:
+        total = total + term
+    return total
 
 
 def apply(ref, vector, add=None):
@@ -309,8 +324,8 @@
                 else:
                     diag[place // 49, place % 49] = tile
     beside = [
-        [from_before(flow[14 + v], 1) for v in range(VARS)],
-        [from_after(flow[21 + v], 1) for v in range(VARS)],
+        [from_before(flow[14 + v]) for v in range(VARS)],
+        [from_after(flow[21 + v]) for v in range(VARS)],
     ]
     source = [
         [-flow[r * VARS + i] - flow[28 + r] * beside[r][i] for i in range(VARS)] for r in range(2)
@@ -331,17 +346,17 @@
             for k in range(VARS):
                 out[i * VARS + k] = total_of([row[j] * b[j * VARS + k] for j in range(VARS)])
 
-    def scan(offset, shifted):
+    def scan(offset, within, eight):
         for level, count in enumerate((1, 2, 4)):
             a = maps.at[level]
             for at in range(49):
-                moved_maps[at] = shifted(a[at], count)
-            offset = apply(a, [shifted(x, count) for x in offset], offset)
+                moved_maps[at] = within(a[at], count, float(at // VARS == at % VARS))
+            offset = apply(a, [within(x, count) for x in offset], offset)
             multiply(a, moved_maps, maps.at[level + 1])
         a = maps.at[3]
         x = offset
         for _ in range(3):
-            x = apply(a, [shifted(part, 8) for part in x], offset)
+            x = apply(a, [eight(part) for part in x], offset)
         return x
 
     times(0, near)
@@ -349,11 +364,11 @@
     first = apply(diag.at[0], source[0])
     second = apply(near.at[1], first, apply(diag.at[1], source[1]))
     multiply(near.at[1], near.at[0], maps.at[0])
-    second = scan(second, from_before)
-    first = apply(near.at[0], [from_before(x, 1) for x in second], first)
+    second = scan(second, within_before, eight_before)
+    first = apply(near.at[0], [from_before(x) for x in second], first)
     multiply(far.at[0], far.at[1], maps.at[0])
-    update_first = scan(apply(far.at[0], second, first), from_after)
-    update_second = apply(far.at[1], [from_after(x, 1) for x in update_first], second)
+    update_first = scan(apply(far.at[0], second, first), within_after, eight_after)
+    update_second = apply(far.at[1], [from_after(x) for x in update_first], second)
 
     results = update_first + update_second + [jnp.zeros((8, 128), F32)] * 2
     for k in range(BACK_ROWS):

time: 89.7 us -> 89.3 us (level)
  no operation moved by 1% of the time
where the time goes in v5:
time: 89.3 us; the launch traced here: 88.9 us
  blocking collectives  31.2 us (35%)
  waiting for transfers between devices  27.3 us (31%)
  starting transfers between devices  22.8 us (26%)
  Pallas kernels  6.73 us (8%)
    all_to_all x2, blocking collectives, exchange(): return lax.all_to_all(shaped, axis, 0, 0, tiled=True).reshape(block.shape)  31.2 us
    all_to_all x1, waiting for transfers between devices, per_device(): moved = lax.all_to_all(send, 'stream', 0, 0, tiled=True)  27.3 us
    all_to_all x1, starting transfers between devices, per_device(): moved = lax.all_to_all(send, 'stream', 0, 0, tiled=True)  17.4 us
    ppermute x1, starting transfers between devices, per_device(): low = lax.ppermute(down, 'stream', ahead)  3.54 us
    pallas_call x1, Pallas kernels, per_device(): pl.pallas_call(flow_kernel, out_shape=(jax.ShapeDtypeStruct((STREAMS, SEN...  2.17 us
    pallas_call x1, Pallas kernels, per_device(): pl.pallas_call(solve_kernel, out_shape=jax.ShapeDtypeStruct((STREAMS * BA...  2.12 us
    ppermute x1, starting transfers between devices, per_device(): high = lax.ppermute(up, 'stream', [(b, a) for a, b in ahead])  1.92 us
  transfers between devices with their start and end apart: 3, of which 1 were waited for; matrix products, arithmetic and copies ran while one was open for 0% of the time, Pallas kernels for 3%

profile of v5, /device:TPU:1, one launch (start us, length us, event | category | flops | bytes accessed | tf_op | source)
XLA Modules:
  0.0 88.9 jit_solution(11563787434704810284)
XLA Ops:
  0.6 1.0 %donors.1 = (f32[384,128]{1,0:T(8,128)S(1)}, f32[7,8,128]{2,1,0:T(8,128)S(1)}) custom-call(f32[7,256]{1,0:T(8,128)} %prop_hbm.1, s32[1,128]{1,0:T(1,128)} %index_hbm.1, s32[1,128]{1,0:T(1,128)} %fringe_hbm.1, f32[1,128]{1,0:T(1,128)} %weight_hbm.1, f32[112,128]{1,0:T(8,128)} %bitcast.8, f32[7]{0:T(128)} %thrust_hbm.1), custom_call_target="tpu_custom_call" | custom-call | tf_op jit(solution)/shard_map/donors/pallas_call | solution.py:423
  1.6 0.0 copy-start.1
  1.6 0.0 copy-start
  1.6 0.0 copy-start.2
  1.6 0.0 copy-start.3
  1.7 0.0 copy-start.4
  1.7 14.7 %all_to_all.15 = f32[16,24,128]{2,1,0:T(8,128)S(1)} all-to-all(f32[16,24,128]{2,1,0:T(8,128)S(1)} %bitcast.9), channel_id=1, replica_groups=mesh['stream'=32,'girth'=16] {'girth'}, dimensions={0} | all-to-all | bytes 393216 | tf_op jit(solution)/shard_map/all_to_all | solution.py:404
  16.4 0.0 copy-done.1
  16.4 0.0 copy-done
  16.4 0.0 copy-done.2
  16.4 0.0 copy-done.3
  16.4 0.0 copy-done.4
  16.4 2.2 %flow.1 = (f32[32,32,128]{2,1,0:T(8,128)}, f32[2,7,8,128]{3,2,1,0:T(8,128)S(1)}, f32[7,8,128]{2,1,0:T(8,128)S(1)}, f32[7,8,128]{2,1,0:T(8,128)S(1)}, f32[2,7,8,1...) custom-call(f32[384,128]{1,0:T(8,128)S(1)} %bitcast.5, f32[2,7,8,128]{3,2,1,0:T(8,128)S(1)} %copy-done, ...), custom_call_target="tpu_custom_call" | custom-call | tf_op jit(solution)/shard_map/flow/pallas_call | solution.py:446
  18.6 0.0 copy-start.6
  18.6 17.4 %all-to-all-start.1 = ((f32[32,32,128]{2,1,0:T(8,128)}), f32[32,32,128]{2,1,0:T(8,128)S(1)}, u32[]{:S(2)}, u32[]{:S(2)}) async-start(f32[32,32,128]{2,1,0:T(8,128)} %get-tuple-element.17), calls=%async_computation.1 | async-start | bytes 1048576 | tf_op jit(solution)/shard_map/all_to_all | solution.py:462
  36.0 0.0 copy-start.5
  36.0 3.5 %collective-permute-start = (f32[7,8,128]{2,1,0:T(8,128)S(1)}, f32[7,8,128]{2,1,0:T(8,128)S(1)}, u32[]{:S(2)}, u32[]{:S(2)}) collective-permute-start(f32[7,8,128]{2,1,0:T(8,128)S(1)} %get-tuple-element.21), channel_id=1, source_target_pairs={{0,16},{16,32},{32,48},{48,64},{64,80},{80,96},{96,112},{112,128},... | collective-permute-start | bytes 86024 | tf_op jit(solution)/shard_map/ppermute | solution.py:464
  39.5 1.9 %collective-permute-start.1 = (f32[7,8,128]{2,1,0:T(8,128)S(1)}, f32[7,8,128]{2,1,0:T(8,128)S(1)}, u32[]{:S(2)}, u32[]{:S(2)}) collective-permute-start(f32[7,8,128]{2,1,0:T(8,128)S(1)} %get-tuple-element.22), channel_id=1, source_target_pairs={{16,0},{32,16},{48,32},{64,48},{80,64},{96,80},{112,96},{128,112},... | collective-permute-start | bytes 86024 | tf_op jit(solution)/shard_map/ppermute | solution.py:465
  41.5 0.0 copy-done.6
  41.5 0.0 copy-done.5
  41.5 0.7 spread.1.spread_ref
  42.2 27.3 %all-to-all-done.1.moved_ref = f32[32,32,128]{2,1,0:T(8,128)S(1)} async-done(((f32[32,32,128]{2,1,0:T(8,128)}), f32[32,32,128]{2,1,0:T(8,128)S(1)}, u32[]{:S(2)}, u32[]{:S(2)}) %all-to-all-start.1) | async-done | bytes 524320 | tf_op jit(solution)/shard_map/all_to_all | solution.py:462
  69.5 2.1 %solve.1 = f32[128,128]{1,0:T(8,128)S(1)} custom-call(f32[32,32,128]{2,1,0:T(8,128)S(1)} %all-to-all-done.1.moved_ref, f32[2,49,8,128]{3,2,1,0:T(8,128)S(1)} %spread.1.spread_ref), custom_call_target="tpu_custom_call" | custom-call | tf_op jit(solution)/shard_map/solve/pallas_call | solution.py:475
  71.6 0.0 collective-permute-done.low_ref
  71.6 0.0 collective-permute-done.1.high_ref
  71.6 16.5 %all_to_all.16 = f32[32,4,128]{2,1,0:T(4,128)S(1)} all-to-all(f32[32,4,128]{2,1,0:T(4,128)S(1)} %bitcast.7), channel_id=1, replica_groups=mesh['stream'=32,'girth'=16] {'stream'}, dimensions={0} | all-to-all | bytes 131072 | tf_op jit(solution)/shard_map/all_to_all | solution.py:404
  88.1 0.8 finish.1
Async XLA Ops:
  1.6 14.8 %copy-start.1 = (bf16[2,7,7,8,128]{4,3,2,1,0:T(8,128)(2,1)S(1)}, bf16[2,7,7,8,128]{4,3,2,1,0:T(8,128)(2,1)}, u32[]{:S(2)}) copy-start(bf16[2,7,7,8,128]{4,3,2,1,0:T(8,128)(2,1)} %diag_ref.1) | copy-start | bytes 602116
  1.6 14.8 %copy-start = (f32[2,7,8,128]{3,2,1,0:T(8,128)S(1)}, f32[2,7,8,128]{3,2,1,0:T(8,128)}, u32[]{:S(2)}) copy-start(f32[2,7,8,128]{3,2,1,0:T(8,128)} %state_ref.1) | copy-start | bytes 172036
  1.6 14.8 %copy-start.2 = (f32[2,6,8,128]{3,2,1,0:T(8,128)S(1)}, f32[2,6,8,128]{3,2,1,0:T(8,128)}, u32[]{:S(2)}) copy-start(f32[2,6,8,128]{3,2,1,0:T(8,128)} %face_ref.1) | copy-start | bytes 147460
  1.6 14.7 %copy-start.3 = (f32[6,7,7]{2,1,0:T(8,128)S(1)}, f32[6,7,7]{2,1,0:T(8,128)}, u32[]{:S(2)}) copy-start(f32[6,7,7]{2,1,0:T(8,128)} %coupling_hbm.1) | copy-start | bytes 3532
  1.7 14.7 %copy-start.4 = (s32[2,8,128]{2,1,0:T(8,128)S(1)}, s32[2,8,128]{2,1,0:T(8,128)}, u32[]{:S(2)}) copy-start(s32[2,8,128]{2,1,0:T(8,128)} %disk_ref.1) | copy-start | bytes 24580
  18.6 22.9 %copy-start.6 = (f32[7,7]{1,0:T(8,128)S(1)}, f32[7,7]{1,0:T(8,128)}, u32[]{:S(2)}) copy-start(f32[7,7]{1,0:T(8,128)} %upper_ref) | copy-start | bytes 592
  18.6 50.9 %all-to-all-start.1 = ((f32[32,32,128]{2,1,0:T(8,128)}), f32[32,32,128]{2,1,0:T(8,128)S(1)}, u32[]{:S(2)}, u32[]{:S(2)}) async-start(f32[32,32,128]{2,1,0:T(8,128)} %get-tuple-element.17), calls=%async_computation.1 | async-start | bytes 1048576 | tf_op jit(solution)/shard_map/all_to_all | solution.py:462
  36.0 5.5 %copy-start.5 = (f32[7,7]{1,0:T(8,128)S(1)}, f32[7,7]{1,0:T(8,128)}, u32[]{:S(2)}) copy-start(f32[7,7]{1,0:T(8,128)} %lower_ref) | copy-start | bytes 592
  36.0 35.6 %collective-permute-start = (f32[7,8,128]{2,1,0:T(8,128)S(1)}, f32[7,8,128]{2,1,0:T(8,128)S(1)}, u32[]{:S(2)}, u32[]{:S(2)}) collective-permute-start(f32[7,8,128]{2,1,0:T(8,128)S(1)} %get-tuple-element.21), channel_id=1, source_target_pairs={{0,16},{16,32},{32,48},{48,64},{64,80},{80,96},{96,112},{112,128},... | collective-permute-start | bytes 86024 | tf_op jit(solution)/shard_map/ppermute | solution.py:464
  39.5 32.1 %collective-permute-start.1 = (f32[7,8,128]{2,1,0:T(8,128)S(1)}, f32[7,8,128]{2,1,0:T(8,128)S(1)}, u32[]{:S(2)}, u32[]{:S(2)}) collective-permute-start(f32[7,8,128]{2,1,0:T(8,128)S(1)} %get-tuple-element.22), channel_id=1, source_target_pairs={{16,0},{32,16},{48,32},{64,48},{80,64},{96,80},{112,96},{128,112},... | collective-permute-start | bytes 86024 | tf_op jit(solution)/shard_map/ppermute | solution.py:465

commit v6 on v5

--- a/solution.py
+++ b/solution.py
@@ -150,12 +150,15 @@
                     rows.append(jnp.where(side == r, marked, 0.0))
             left[which, group] = jnp.concatenate(rows, axis=0).astype(BF16)
     right = jnp.concatenate(right, axis=1)
-    total = None
-    for which in range(3):
-        lhs = jnp.concatenate([left[which, group] for group in range(4)], axis=1)
-        part = lax.dot_general(lhs, right, (((1,), (1,)), ((), ())), preferred_element_type=F32)
-        total = part if total is None else total + part
-    return total
+    lhs = jnp.concatenate(
+        [
+            jnp.concatenate([left[which, group] for group in range(4)], axis=1)
+            for which in range(3)
+        ],
+        axis=0,
+    )
+    sums = lax.dot_general(lhs, right, (((1,), (1,)), ((), ())), preferred_element_type=F32)
+    return sums[0:160, :] + sums[160:320, :] + sums[320:480, :]
 
 
 def flow_kernel(
@@ -276,13 +279,13 @@
 
 
 def eight_before(x):
-    x = jnp.where(lanes() < 32, 0.0, pltpu.roll(x, 32, 1))
-    return jnp.broadcast_to(x[7:8, :], (8, 128))
+    x = jnp.broadcast_to(x[7:8, :], (8, 128))
+    return jnp.where(lanes() < 32, 0.0, pltpu.roll(x, 32, 1))
 
 
 def eight_after(x):
-    x = jnp.where(lanes() >= 96, 0.0, pltpu.roll(x, 96, 1))
-    return jnp.broadcast_to(x[0:1, :], (8, 128))
+    x = jnp.broadcast_to(x[0:1, :], (8, 128))
+    return jnp.where(lanes() >= 96, 0.0, pltpu.roll(x, 96, 1))
 
 
 def total_of(terms):

time: 89.3 us -> 89.3 us (level)
  no operation moved by 1% of the time
where the time goes in v6:
time: 89.3 us; the launch traced here: 88.9 us
  blocking collectives  31.2 us (35%)
  waiting for transfers between devices  27.3 us (31%)
  starting transfers between devices  22.8 us (26%)
  Pallas kernels  6.74 us (8%)
    all_to_all x2, blocking collectives, exchange(): return lax.all_to_all(shaped, axis, 0, 0, tiled=True).reshape(block.shape)  31.2 us
    all_to_all x1, waiting for transfers between devices, per_device(): moved = lax.all_to_all(send, 'stream', 0, 0, tiled=True)  27.3 us
    all_to_all x1, starting transfers between devices, per_device(): moved = lax.all_to_all(send, 'stream', 0, 0, tiled=True)  17.4 us
    ppermute x1, starting transfers between devices, per_device(): low = lax.ppermute(down, 'stream', ahead)  3.54 us
    pallas_call x1, Pallas kernels, per_device(): pl.pallas_call(flow_kernel, out_shape=(jax.ShapeDtypeStruct((STREAMS, SEN...  2.16 us
    pallas_call x1, Pallas kernels, per_device(): pl.pallas_call(solve_kernel, out_shape=jax.ShapeDtypeStruct((STREAMS * BA...  2.13 us
    ppermute x1, starting transfers between devices, per_device(): high = lax.ppermute(up, 'stream', [(b, a) for a, b in ahead])  1.92 us
  transfers between devices with their start and end apart: 3, of which 1 were waited for; matrix products, arithmetic and copies ran while one was open for 0% of the time, Pallas kernels for 3%

profile of v6, /device:TPU:1, one launch (start us, length us, event | category | flops | bytes accessed | tf_op | source)
XLA Modules:
  0.0 88.9 jit_solution(1614703789018295056)
XLA Ops:
  0.6 1.0 %donors.1 = (f32[384,128]{1,0:T(8,128)S(1)}, f32[7,8,128]{2,1,0:T(8,128)S(1)}) custom-call(f32[7,256]{1,0:T(8,128)} %prop_hbm.1, s32[1,128]{1,0:T(1,128)} %index_hbm.1, s32[1,128]{1,0:T(1,128)} %fringe_hbm.1, f32[1,128]{1,0:T(1,128)} %weight_hbm.1, f32[112,128]{1,0:T(8,128)} %bitcast.8, f32[7]{0:T(128)} %thrust_hbm.1), custom_call_target="tpu_custom_call" | custom-call | tf_op jit(solution)/shard_map/donors/pallas_call | solution.py:426
  1.6 0.0 copy-start.1
  1.6 0.0 copy-start
  1.6 0.0 copy-start.2
  1.6 0.0 copy-start.3
  1.7 0.0 copy-start.4
  1.7 14.7 %all_to_all.15 = f32[16,24,128]{2,1,0:T(8,128)S(1)} all-to-all(f32[16,24,128]{2,1,0:T(8,128)S(1)} %bitcast.9), channel_id=1, replica_groups=mesh['stream'=32,'girth'=16] {'girth'}, dimensions={0} | all-to-all | bytes 393216 | tf_op jit(solution)/shard_map/all_to_all | solution.py:407
  16.4 0.0 copy-done.1
  16.4 0.0 copy-done
  16.4 0.0 copy-done.2
  16.4 0.0 copy-done.3
  16.4 0.0 copy-done.4
  16.4 2.2 %flow.1 = (f32[32,32,128]{2,1,0:T(8,128)}, f32[2,7,8,128]{3,2,1,0:T(8,128)S(1)}, f32[7,8,128]{2,1,0:T(8,128)S(1)}, f32[7,8,128]{2,1,0:T(8,128)S(1)}, f32[2,7,8,1...) custom-call(f32[384,128]{1,0:T(8,128)S(1)} %bitcast.5, f32[2,7,8,128]{3,2,1,0:T(8,128)S(1)} %copy-done, ...), custom_call_target="tpu_custom_call" | custom-call | tf_op jit(solution)/shard_map/flow/pallas_call | solution.py:449
  18.6 0.0 copy-start.6
  18.6 17.4 %all-to-all-start.1 = ((f32[32,32,128]{2,1,0:T(8,128)}), f32[32,32,128]{2,1,0:T(8,128)S(1)}, u32[]{:S(2)}, u32[]{:S(2)}) async-start(f32[32,32,128]{2,1,0:T(8,128)} %get-tuple-element.17), calls=%async_computation.1 | async-start | bytes 1048576 | tf_op jit(solution)/shard_map/all_to_all | solution.py:465
  36.0 0.0 copy-start.5
  36.0 3.5 %collective-permute-start = (f32[7,8,128]{2,1,0:T(8,128)S(1)}, f32[7,8,128]{2,1,0:T(8,128)S(1)}, u32[]{:S(2)}, u32[]{:S(2)}) collective-permute-start(f32[7,8,128]{2,1,0:T(8,128)S(1)} %get-tuple-element.21), channel_id=1, source_target_pairs={{0,16},{16,32},{32,48},{48,64},{64,80},{80,96},{96,112},{112,128},... | collective-permute-start | bytes 86024 | tf_op jit(solution)/shard_map/ppermute | solution.py:467
  39.5 1.9 %collective-permute-start.1 = (f32[7,8,128]{2,1,0:T(8,128)S(1)}, f32[7,8,128]{2,1,0:T(8,128)S(1)}, u32[]{:S(2)}, u32[]{:S(2)}) collective-permute-start(f32[7,8,128]{2,1,0:T(8,128)S(1)} %get-tuple-element.22), channel_id=1, source_target_pairs={{16,0},{32,16},{48,32},{64,48},{80,64},{96,80},{112,96},{128,112},... | collective-permute-start | bytes 86024 | tf_op jit(solution)/shard_map/ppermute | solution.py:468
  41.5 0.0 copy-done.6
  41.5 0.0 copy-done.5
  41.5 0.7 spread.1.spread_ref
  42.2 27.3 %all-to-all-done.1.moved_ref = f32[32,32,128]{2,1,0:T(8,128)S(1)} async-done(((f32[32,32,128]{2,1,0:T(8,128)}), f32[32,32,128]{2,1,0:T(8,128)S(1)}, u32[]{:S(2)}, u32[]{:S(2)}) %all-to-all-start.1) | async-done | bytes 524320 | tf_op jit(solution)/shard_map/all_to_all | solution.py:465
  69.5 2.1 %solve.1 = f32[128,128]{1,0:T(8,128)S(1)} custom-call(f32[32,32,128]{2,1,0:T(8,128)S(1)} %all-to-all-done.1.moved_ref, f32[2,49,8,128]{3,2,1,0:T(8,128)S(1)} %spread.1.spread_ref), custom_call_target="tpu_custom_call" | custom-call | tf_op jit(solution)/shard_map/solve/pallas_call | solution.py:478
  71.6 0.0 collective-permute-done.low_ref
  71.6 0.0 collective-permute-done.1.high_ref
  71.6 16.5 %all_to_all.16 = f32[32,4,128]{2,1,0:T(4,128)S(1)} all-to-all(f32[32,4,128]{2,1,0:T(4,128)S(1)} %bitcast.7), channel_id=1, replica_groups=mesh['stream'=32,'girth'=16] {'stream'}, dimensions={0} | all-to-all | bytes 131072 | tf_op jit(solution)/shard_map/all_to_all | solution.py:407
  88.1 0.8 finish.1
Async XLA Ops:
  1.6 14.8 %copy-start.1 = (bf16[2,7,7,8,128]{4,3,2,1,0:T(8,128)(2,1)S(1)}, bf16[2,7,7,8,128]{4,3,2,1,0:T(8,128)(2,1)}, u32[]{:S(2)}) copy-start(bf16[2,7,7,8,128]{4,3,2,1,0:T(8,128)(2,1)} %diag_ref.1) | copy-start | bytes 602116
  1.6 14.8 %copy-start = (f32[2,7,8,128]{3,2,1,0:T(8,128)S(1)}, f32[2,7,8,128]{3,2,1,0:T(8,128)}, u32[]{:S(2)}) copy-start(f32[2,7,8,128]{3,2,1,0:T(8,128)} %state_ref.1) | copy-start | bytes 172036
  1.6 14.8 %copy-start.2 = (f32[2,6,8,128]{3,2,1,0:T(8,128)S(1)}, f32[2,6,8,128]{3,2,1,0:T(8,128)}, u32[]{:S(2)}) copy-start(f32[2,6,8,128]{3,2,1,0:T(8,128)} %face_ref.1) | copy-start | bytes 147460
  1.6 14.7 %copy-start.3 = (f32[6,7,7]{2,1,0:T(8,128)S(1)}, f32[6,7,7]{2,1,0:T(8,128)}, u32[]{:S(2)}) copy-start(f32[6,7,7]{2,1,0:T(8,128)} %coupling_hbm.1) | copy-start | bytes 3532
  1.7 14.7 %copy-start.4 = (s32[2,8,128]{2,1,0:T(8,128)S(1)}, s32[2,8,128]{2,1,0:T(8,128)}, u32[]{:S(2)}) copy-start(s32[2,8,128]{2,1,0:T(8,128)} %disk_ref.1) | copy-start | bytes 24580
  18.6 22.9 %copy-start.6 = (f32[7,7]{1,0:T(8,128)S(1)}, f32[7,7]{1,0:T(8,128)}, u32[]{:S(2)}) copy-start(f32[7,7]{1,0:T(8,128)} %upper_ref) | copy-start | bytes 592
  18.6 50.9 %all-to-all-start.1 = ((f32[32,32,128]{2,1,0:T(8,128)}), f32[32,32,128]{2,1,0:T(8,128)S(1)}, u32[]{:S(2)}, u32[]{:S(2)}) async-start(f32[32,32,128]{2,1,0:T(8,128)} %get-tuple-element.17), calls=%async_computation.1 | async-start | bytes 1048576 | tf_op jit(solution)/shard_map/all_to_all | solution.py:465
  36.0 5.5 %copy-start.5 = (f32[7,7]{1,0:T(8,128)S(1)}, f32[7,7]{1,0:T(8,128)}, u32[]{:S(2)}) copy-start(f32[7,7]{1,0:T(8,128)} %lower_ref) | copy-start | bytes 592
  36.0 35.6 %collective-permute-start = (f32[7,8,128]{2,1,0:T(8,128)S(1)}, f32[7,8,128]{2,1,0:T(8,128)S(1)}, u32[]{:S(2)}, u32[]{:S(2)}) collective-permute-start(f32[7,8,128]{2,1,0:T(8,128)S(1)} %get-tuple-element.21), channel_id=1, source_target_pairs={{0,16},{16,32},{32,48},{48,64},{64,80},{80,96},{96,112},{112,128},... | collective-permute-start | bytes 86024 | tf_op jit(solution)/shard_map/ppermute | solution.py:467
  39.5 32.1 %collective-permute-start.1 = (f32[7,8,128]{2,1,0:T(8,128)S(1)}, f32[7,8,128]{2,1,0:T(8,128)S(1)}, u32[]{:S(2)}, u32[]{:S(2)}) collective-permute-start(f32[7,8,128]{2,1,0:T(8,128)S(1)} %get-tuple-element.22), channel_id=1, source_target_pairs={{16,0},{32,16},{48,32},{64,48},{80,64},{96,80},{112,96},{128,112},... | collective-permute-start | bytes 86024 | tf_op jit(solution)/shard_map/ppermute | solution.py:468

commit v7 on v6

--- a/solution.py
+++ b/solution.py
@@ -88,9 +88,10 @@
     index = index_ref[...]
     cells = lax.broadcasted_iota(jnp.int32, (256, 128), 0)
     pick = jnp.where(cells == index, 1.0, 0.0).astype(BF16)
-    values = jnp.zeros((VARS, 128), F32)
-    for part in split_parts(prop_ref[...]):
-        values = values + jnp.dot(part.astype(BF16), pick, preferred_element_type=F32)
+    pad = jnp.zeros((1, 256), F32)
+    parts = [jnp.concatenate([part, pad], axis=0) for part in split_parts(prop_ref[...])]
+    sums = jnp.dot(jnp.concatenate(parts, axis=0).astype(BF16), pick, preferred_element_type=F32)
+    values = (sums[0:8, :] + sums[8:16, :] + sums[16:24, :])[:VARS, :]
     for copy in copies[2:]:
         copy.wait()
     values = values * weight_ref[...]

time: 89.3 us -> 89.3 us (level)
  no operation moved by 1% of the time
where the time goes in v7:
time: 89.3 us; the launch traced here: 88.9 us
  blocking collectives  31.2 us (35%)
  waiting for transfers between devices  27.3 us (31%)
  starting transfers between devices  22.8 us (26%)
  Pallas kernels  6.74 us (8%)
    all_to_all x2, blocking collectives, exchange(): return lax.all_to_all(shaped, axis, 0, 0, tiled=True).reshape(block.shape)  31.2 us
    all_to_all x1, waiting for transfers between devices, per_device(): moved = lax.all_to_all(send, 'stream', 0, 0, tiled=True)  27.3 us
    all_to_all x1, starting transfers between devices, per_device(): moved = lax.all_to_all(send, 'stream', 0, 0, tiled=True)  17.4 us
    ppermute x1, starting transfers between devices, per_device(): low = lax.ppermute(down, 'stream', ahead)  3.54 us
    pallas_call x1, Pallas kernels, per_device(): pl.pallas_call(flow_kernel, out_shape=(jax.ShapeDtypeStruct((STREAMS, SEN...  2.16 us
    pallas_call x1, Pallas kernels, per_device(): pl.pallas_call(solve_kernel, out_shape=jax.ShapeDtypeStruct((STREAMS * BA...  2.13 us
    ppermute x1, starting transfers between devices, per_device(): high = lax.ppermute(up, 'stream', [(b, a) for a, b in ahead])  1.92 us
  transfers between devices with their start and end apart: 3, of which 1 were waited for; matrix products, arithmetic and copies ran while one was open for 0% of the time, Pallas kernels for 3%

profile of v7, /device:TPU:1, one launch (start us, length us, event | category | flops | bytes accessed | tf_op | source)
XLA Modules:
  0.0 88.9 jit_solution(15194158481599180729)
XLA Ops:
  0.6 1.0 %donors.1 = (f32[384,128]{1,0:T(8,128)S(1)}, f32[7,8,128]{2,1,0:T(8,128)S(1)}) custom-call(f32[7,256]{1,0:T(8,128)} %prop_hbm.1, s32[1,128]{1,0:T(1,128)} %index_hbm.1, s32[1,128]{1,0:T(1,128)} %fringe_hbm.1, f32[1,128]{1,0:T(1,128)} %weight_hbm.1, f32[112,128]{1,0:T(8,128)} %bitcast.8, f32[7]{0:T(128)} %thrust_hbm.1), custom_call_target="tpu_custom_call" | custom-call | tf_op jit(solution)/shard_map/donors/pallas_call | solution.py:427
  1.6 0.0 copy-start.1
  1.6 0.0 copy-start
  1.6 0.0 copy-start.2
  1.6 0.0 copy-start.3
  1.7 0.0 copy-start.4
  1.7 14.7 %all_to_all.15 = f32[16,24,128]{2,1,0:T(8,128)S(1)} all-to-all(f32[16,24,128]{2,1,0:T(8,128)S(1)} %bitcast.9), channel_id=1, replica_groups=mesh['stream'=32,'girth'=16] {'girth'}, dimensions={0} | all-to-all | bytes 393216 | tf_op jit(solution)/shard_map/all_to_all | solution.py:408
  16.4 0.0 copy-done.1
  16.4 0.0 copy-done
  16.4 0.0 copy-done.2
  16.4 0.0 copy-done.3
  16.4 0.0 copy-done.4
  16.4 2.2 %flow.1 = (f32[32,32,128]{2,1,0:T(8,128)}, f32[2,7,8,128]{3,2,1,0:T(8,128)S(1)}, f32[7,8,128]{2,1,0:T(8,128)S(1)}, f32[7,8,128]{2,1,0:T(8,128)S(1)}, f32[2,7,8,1...) custom-call(f32[384,128]{1,0:T(8,128)S(1)} %bitcast.5, f32[2,7,8,128]{3,2,1,0:T(8,128)S(1)} %copy-done, ...), custom_call_target="tpu_custom_call" | custom-call | tf_op jit(solution)/shard_map/flow/pallas_call | solution.py:450
  18.6 0.0 copy-start.6
  18.6 17.4 %all-to-all-start.1 = ((f32[32,32,128]{2,1,0:T(8,128)}), f32[32,32,128]{2,1,0:T(8,128)S(1)}, u32[]{:S(2)}, u32[]{:S(2)}) async-start(f32[32,32,128]{2,1,0:T(8,128)} %get-tuple-element.17), calls=%async_computation.1 | async-start | bytes 1048576 | tf_op jit(solution)/shard_map/all_to_all | solution.py:466
  36.0 0.0 copy-start.5
  36.0 3.5 %collective-permute-start = (f32[7,8,128]{2,1,0:T(8,128)S(1)}, f32[7,8,128]{2,1,0:T(8,128)S(1)}, u32[]{:S(2)}, u32[]{:S(2)}) collective-permute-start(f32[7,8,128]{2,1,0:T(8,128)S(1)} %get-tuple-element.21), channel_id=1, source_target_pairs={{0,16},{16,32},{32,48},{48,64},{64,80},{80,96},{96,112},{112,128},... | collective-permute-start | bytes 86024 | tf_op jit(solution)/shard_map/ppermute | solution.py:468
  39.5 1.9 %collective-permute-start.1 = (f32[7,8,128]{2,1,0:T(8,128)S(1)}, f32[7,8,128]{2,1,0:T(8,128)S(1)}, u32[]{:S(2)}, u32[]{:S(2)}) collective-permute-start(f32[7,8,128]{2,1,0:T(8,128)S(1)} %get-tuple-element.22), channel_id=1, source_target_pairs={{16,0},{32,16},{48,32},{64,48},{80,64},{96,80},{112,96},{128,112},... | collective-permute-start | bytes 86024 | tf_op jit(solution)/shard_map/ppermute | solution.py:469
  41.5 0.0 copy-done.6
  41.5 0.0 copy-done.5
  41.5 0.7 spread.1.spread_ref
  42.2 27.3 %all-to-all-done.1.moved_ref = f32[32,32,128]{2,1,0:T(8,128)S(1)} async-done(((f32[32,32,128]{2,1,0:T(8,128)}), f32[32,32,128]{2,1,0:T(8,128)S(1)}, u32[]{:S(2)}, u32[]{:S(2)}) %all-to-all-start.1) | async-done | bytes 524320 | tf_op jit(solution)/shard_map/all_to_all | solution.py:466
  69.5 2.1 %solve.1 = f32[128,128]{1,0:T(8,128)S(1)} custom-call(f32[32,32,128]{2,1,0:T(8,128)S(1)} %all-to-all-done.1.moved_ref, f32[2,49,8,128]{3,2,1,0:T(8,128)S(1)} %spread.1.spread_ref), custom_call_target="tpu_custom_call" | custom-call | tf_op jit(solution)/shard_map/solve/pallas_call | solution.py:479
  71.6 0.0 collective-permute-done.low_ref
  71.6 0.0 collective-permute-done.1.high_ref
  71.6 16.5 %all_to_all.16 = f32[32,4,128]{2,1,0:T(4,128)S(1)} all-to-all(f32[32,4,128]{2,1,0:T(4,128)S(1)} %bitcast.7), channel_id=1, replica_groups=mesh['stream'=32,'girth'=16] {'stream'}, dimensions={0} | all-to-all | bytes 131072 | tf_op jit(solution)/shard_map/all_to_all | solution.py:408
  88.1 0.8 finish.1
Async XLA Ops:
  1.6 14.8 %copy-start.1 = (bf16[2,7,7,8,128]{4,3,2,1,0:T(8,128)(2,1)S(1)}, bf16[2,7,7,8,128]{4,3,2,1,0:T(8,128)(2,1)}, u32[]{:S(2)}) copy-start(bf16[2,7,7,8,128]{4,3,2,1,0:T(8,128)(2,1)} %diag_ref.1) | copy-start | bytes 602116
  1.6 14.8 %copy-start = (f32[2,7,8,128]{3,2,1,0:T(8,128)S(1)}, f32[2,7,8,128]{3,2,1,0:T(8,128)}, u32[]{:S(2)}) copy-start(f32[2,7,8,128]{3,2,1,0:T(8,128)} %state_ref.1) | copy-start | bytes 172036
  1.6 14.8 %copy-start.2 = (f32[2,6,8,128]{3,2,1,0:T(8,128)S(1)}, f32[2,6,8,128]{3,2,1,0:T(8,128)}, u32[]{:S(2)}) copy-start(f32[2,6,8,128]{3,2,1,0:T(8,128)} %face_ref.1) | copy-start | bytes 147460
  1.6 14.7 %copy-start.3 = (f32[6,7,7]{2,1,0:T(8,128)S(1)}, f32[6,7,7]{2,1,0:T(8,128)}, u32[]{:S(2)}) copy-start(f32[6,7,7]{2,1,0:T(8,128)} %coupling_hbm.1) | copy-start | bytes 3532
  1.7 14.7 %copy-start.4 = (s32[2,8,128]{2,1,0:T(8,128)S(1)}, s32[2,8,128]{2,1,0:T(8,128)}, u32[]{:S(2)}) copy-start(s32[2,8,128]{2,1,0:T(8,128)} %disk_ref.1) | copy-start | bytes 24580
  18.6 22.9 %copy-start.6 = (f32[7,7]{1,0:T(8,128)S(1)}, f32[7,7]{1,0:T(8,128)}, u32[]{:S(2)}) copy-start(f32[7,7]{1,0:T(8,128)} %upper_ref) | copy-start | bytes 592
  18.6 50.9 %all-to-all-start.1 = ((f32[32,32,128]{2,1,0:T(8,128)}), f32[32,32,128]{2,1,0:T(8,128)S(1)}, u32[]{:S(2)}, u32[]{:S(2)}) async-start(f32[32,32,128]{2,1,0:T(8,128)} %get-tuple-element.17), calls=%async_computation.1 | async-start | bytes 1048576 | tf_op jit(solution)/shard_map/all_to_all | solution.py:466
  36.0 5.5 %copy-start.5 = (f32[7,7]{1,0:T(8,128)S(1)}, f32[7,7]{1,0:T(8,128)}, u32[]{:S(2)}) copy-start(f32[7,7]{1,0:T(8,128)} %lower_ref) | copy-start | bytes 592
  36.0 35.6 %collective-permute-start = (f32[7,8,128]{2,1,0:T(8,128)S(1)}, f32[7,8,128]{2,1,0:T(8,128)S(1)}, u32[]{:S(2)}, u32[]{:S(2)}) collective-permute-start(f32[7,8,128]{2,1,0:T(8,128)S(1)} %get-tuple-element.21), channel_id=1, source_target_pairs={{0,16},{16,32},{32,48},{48,64},{64,80},{80,96},{96,112},{112,128},... | collective-permute-start | bytes 86024 | tf_op jit(solution)/shard_map/ppermute | solution.py:468
  39.5 32.1 %collective-permute-start.1 = (f32[7,8,128]{2,1,0:T(8,128)S(1)}, f32[7,8,128]{2,1,0:T(8,128)S(1)}, u32[]{:S(2)}, u32[]{:S(2)}) collective-permute-start(f32[7,8,128]{2,1,0:T(8,128)S(1)} %get-tuple-element.22), channel_id=1, source_target_pairs={{16,0},{32,16},{48,32},{64,48},{80,64},{96,80},{112,96},{128,112},... | collective-permute-start | bytes 86024 | tf_op jit(solution)/shard_map/ppermute | solution.py:469
